TPU v7x, 512 devices: a whole 4x4x16 slice. The times are simulated.
512 devices in a mesh: mem: 16 (over z_hi, y), reg: 32 (over x, z_lo, core).
Axes of the slice: x: 4, y: 4, z: 16 (z_hi: 4, z_lo: 4; z = z_hi * 4 + z_lo), core: 2. Of those that a mesh axis runs over, the one named last changes fastest.
Arguments:
- alpha: float32 [128, 16, 128, 128], P('mem', None, 'reg'), may hold values from -6 to 6
- perturbation: bfloat16 [128, 2, 16, 512, 512], P('mem', None, None, 'reg'), may hold values from -6 to 6
- obs_cell: int32 [32768], P('reg'), may hold values from 0 to 131071
- obs_kind: int32 [32768], P('reg'), may hold values from 0 to 3
- obs_value: float32 [32768], P('reg'), may hold values from -6 to 6
- obs_weight: float32 [32768], P('reg'), may hold values from 1 to 4
Outputs:
- obs_gradient: float32 [128, 16, 128, 128], P('mem', None, 'reg')
Inputs may be any that keep to these rules, and one draw needn't show every extreme that they name: `obs_cell`: each entry is level * 16 * 512 + row * 512 + column of a fine cell, the row counted from the first row of the observation's own region. `obs_kind`: 0 zonal wind, 1 meridional wind, 2 relative vorticity, 3 zonal wind advection.
All inputs are finite; a program needn't handle non-finite values.
Results may differ from a plain program's by a relative error of at most 0.0003.
Values sent between devices are 32-bit elements; how exact they have to be, the bound alone decides.
A program may use at most 64 MiB of HBM per device.

v0:
```python
import math

import jax
import jax.numpy as jnp
from jax import lax
from jax.sharding import PartitionSpec as P

PASSES = 2


diffuse = 0.2
highest = lax.Precision.HIGHEST


def padded_2(value, sides, width):
    for axis, dim in sides:
        devices, length = (lax.axis_size(axis), value.shape[dim])
        up = [(i, (i + 1) % devices) for i in range(devices - 1)]
        down = [(j, i) for i, j in up]
        last = lax.slice_in_dim(value, length - width, length, axis=dim)
        first = lax.slice_in_dim(value, 0, width, axis=dim)
        before = lax.ppermute(last, axis, up)
        after = lax.ppermute(first, axis, down)
        value = jnp.concatenate([before, value, after], axis=dim)
    return value


def cut_along(value, dim, devices):
    dims = value.shape
    parts = value.reshape(*dims[:dim], devices, dims[dim] // devices, *dims[dim + 1 :])
    return jnp.moveaxis(parts, dim, 0)


def sum_at_owner(value, axis, dim):
    devices = lax.axis_size(axis)
    parts = lax.all_to_all(cut_along(value, dim, devices), axis, 0, 0, tiled=True)
    return jnp.sum(parts, axis=0)


def from_everyone(value, axis):
    devices = lax.axis_size(axis)
    return lax.all_to_all(
        jnp.broadcast_to(value[None], (devices, *value.shape)), axis, 0, 0, tiled=True
    )


def in_order(parts, dim):
    dims = list(parts.shape[1:])
    dims[dim] *= parts.shape[0]
    return jnp.moveaxis(parts, 0, dim).reshape(dims)


def gathered_copies(value, axis, dim):
    parts = from_everyone(value, axis)
    return in_order(parts, dim)


def from_behind(value, axis, by):
    devices = lax.axis_size(axis)
    pairs = [(i, i + by) for i in range(devices) if 0 <= i + by < devices]
    return lax.ppermute(value, axis, pairs)


def weights(fine_rows, fine_start, coarse_count, coarse_start):
    finer = (jnp.arange(fine_rows) + fine_start).astype(jnp.float32)
    coarser = (jnp.arange(coarse_count) + coarse_start).astype(jnp.float32)
    where_at = (finer[:, None] + 0.5) / 4.0 - 0.5
    return jnp.maximum(0.0, 1.0 - jnp.abs(where_at - coarser[None, :]))


def one_pass(block):
    padded = jnp.pad(block, ((0, 0), (0, 0), (1, 1), (1, 1)))
    beside_all = (
        padded[:, :, 2:, 1:-1]
        + padded[:, :, :-2, 1:-1]
        + padded[:, :, 1:-1, 2:]
        + padded[:, :, 1:-1, :-2]
    )
    return block + diffuse * (beside_all - 4.0 * block)


def slopes(padded):
    along_x = (padded[..., 2:, 1:-1] - padded[..., :-2, 1:-1]) * 0.5
    along_y = (padded[..., 1:-1, 2:] - padded[..., 1:-1, :-2]) * 0.5
    return (along_x, along_y)


def mask_rows(block, first_row, total_rows):
    rows_here = first_row + jnp.arange(block.shape[2])
    keeping = (rows_here >= 0) & (rows_here < total_rows)
    return jnp.where(keeping[None, None, :, None], block, 0.0)


def smooth_rows(block, passes, keep):
    region = lax.axis_index("reg")
    total_rows = block.shape[2] * lax.axis_size("reg")
    extended = padded_2(block, (("reg", 2),), passes + keep)
    first_row = region * block.shape[2] - passes - keep
    for step in range(passes):
        extended = one_pass(extended)[:, :, 1:-1, :]
        first_row = first_row + 1
        extended = mask_rows(extended, first_row, total_rows)
    return extended


def observe(extended, level_first, obs_cell, obs_kind, obs_value, obs_weight, back_rim):
    levels = extended.shape[1]
    rows = extended.shape[2] - 2
    fine_cols = extended.shape[3] - 2
    zonal_x, zonal_y = slopes(extended[0])
    merid_x, _ = slopes(extended[1])
    zonal = extended[0, :, 1:-1, 1:-1]
    merid = extended[1, :, 1:-1, 1:-1]
    fields = jnp.stack([zonal, merid, merid_x - zonal_y, zonal * zonal_x + merid * zonal_y])
    plane = rows * fine_cols
    level = obs_cell // plane
    rest = obs_cell % plane
    row_in = rest // fine_cols
    column = rest % fine_cols
    inside = (level >= level_first) & (level < level_first + levels)
    local_level = jnp.clip(level - level_first, 0, levels - 1)
    line_count = 4 * levels * rows
    line = obs_kind * (levels * rows) + local_level * rows + row_in
    line_hot = (line[:, None] == jnp.arange(line_count, dtype=jnp.int32)[None, :]).astype(
        jnp.float32
    )
    column_hot = (column[:, None] == jnp.arange(fine_cols, dtype=jnp.int32)[None, :]).astype(
        jnp.float32
    )
    table = fields.reshape(line_count, fine_cols)
    picked = jnp.dot(line_hot, table, precision=highest, preferred_element_type=jnp.float32)
    seen = jnp.sum(picked * column_hot, axis=1)
    misfit = jnp.where(inside, obs_weight * (seen - obs_value), 0.0)
    weighted = misfit[:, None] * column_hot
    adjoint = lax.dot_general(
        line_hot,
        weighted,
        (((0,), (0,)), ((), ())),
        precision=highest,
        preferred_element_type=jnp.float32,
    )
    adjoint = adjoint.reshape(4, levels, rows, fine_cols)
    back = back_rim(jnp.stack([adjoint[2], adjoint[3] * zonal, adjoint[3] * merid]))
    vort_x, vort_y = slopes(back[0])
    flux_x, _ = slopes(back[1])
    _, flux_y = slopes(back[2])
    grad_u = adjoint[0] + adjoint[3] * zonal_x + vort_y - flux_x - flux_y
    grad_v = adjoint[1] + adjoint[3] * zonal_y - vort_x
    return jnp.stack([grad_u, grad_v])


def local(alpha, perturbation, obs_cell, obs_kind, obs_value, obs_weight):
    members, levels, coarse_rows, coarse_cols = alpha.shape
    fine_rows = perturbation.shape[3]
    region = lax.axis_index("reg")
    scale = 1.0 / math.sqrt(members * lax.axis_size("mem"))
    rows_x = weights(fine_rows, region * fine_rows, coarse_rows + 2, region * coarse_rows - 1)
    rows_y = weights(perturbation.shape[4], 0, coarse_cols, 0)
    smoothed = smooth_rows(alpha, PASSES, 1)
    part = jnp.einsum("ia,mlab->mlib", rows_x, smoothed, precision=highest)
    fine = jnp.einsum("mlib,jb->mlij", part, rows_y, precision=highest)
    partial_value = jnp.sum(fine[:, None] * perturbation.astype(jnp.float32), axis=0) * scale
    share = sum_at_owner(partial_value, "mem", 1)
    level_first = lax.axis_index("mem") * share.shape[1]
    rimmed_share = padded_2(share, (("reg", 2),), 1)
    extended = jnp.pad(rimmed_share, ((0, 0), (0, 0), (0, 0), (1, 1)))

    def back_rim(carried):
        rimmed_rows = padded_2(carried, (("reg", 2),), 1)
        return jnp.pad(rimmed_rows, ((0, 0), (0, 0), (0, 0), (1, 1)))

    grad_fine = observe(extended, level_first, obs_cell, obs_kind, obs_value, obs_weight, back_rim)
    product = jnp.sum(
        perturbation.astype(jnp.float32) * gathered_copies(grad_fine, "mem", 1)[None], axis=1
    )
    projected_part = jnp.einsum("mlij,jb->mlib", product, rows_y, precision=highest)
    coarse = jnp.einsum("ia,mlib->mlab", rows_x, projected_part, precision=highest) * scale
    from_above = from_behind(coarse[:, :, 0], "reg", -1)
    from_below = from_behind(coarse[:, :, -1], "reg", 1)
    inner = coarse[:, :, 1:-1]
    inner = inner.at[:, :, -1].add(from_above)
    inner = inner.at[:, :, 0].add(from_below)
    return smooth_rows(inner, PASSES, 0)


def solution(mesh):
    return jax.shard_map(
        local,
        mesh=mesh,
        in_specs=(
            P("mem", None, "reg", None),
            P("mem", None, None, "reg", None),
            P("reg"),
            P("reg"),
            P("reg"),
            P("reg"),
        ),
        out_specs=P("mem", None, "reg", None),
        check_vma=False,
    )
```

profile of v0, /device:TPU:99, one launch (start us, length us, event | category | flops | bytes accessed | tf_op | source)
XLA Modules:
  0.0 204.4 jit_solution(2357327350353129958)
XLA Ops:
  0.0 1.2 fusion.91
  1.2 2.3 %collective-permute-start = (f32[8,16,3,128]{3,1,0,2:T(8,128)S(1)}, f32[8,16,3,128]{3,1,0,2:T(8,128)S(1)}, u32[]{:S(2)}, u32[]{:S(2)}) collective-permute-start(f32[8,16,3,128]{3,1,0,2:T(8,128)S(1)} %copy.40), channel_id=1, source_target_pairs={{0,1},{1,2},{2,3},{3,4},{4,5},{5,6},{6,7},{7,8},{8,9},{9,10},{10,1... | collective-permute-start | bytes 589832 | tf_op jit(solution)/shard_map/ppermute | solution.py:22
  3.6 2.2 %collective-permute-start.1 = (f32[8,16,3,128]{3,1,0,2:T(8,128)S(1)}, f32[8,16,3,128]{3,1,0,2:T(8,128)S(1)}, u32[]{:S(2)}, u32[]{:S(2)}) collective-permute-start(f32[8,16,3,128]{3,1,0,2:T(8,128)S(1)} %copy.41), channel_id=1, source_target_pairs={{1,0},{2,1},{3,2},{4,3},{5,4},{6,5},{7,6},{8,7},{9,8},{10,9},{11,1... | collective-permute-start | bytes 589832 | tf_op jit(solution)/shard_map/ppermute | solution.py:23
  6.2 7.1 %collective-permute-done.1 = f32[8,16,3,128]{3,1,0,2:T(8,128)S(1)} collective-permute-done((f32[8,16,3,128]{3,1,0,2:T(8,128)S(1)}, f32[8,16,3,128]{3,1,0,2:T(8,128)S(1)}, u32[]{:S(2)}, u32[]{:S(2)}) %collective-permute-start.1) | collective-permute-done | bytes 196640 | tf_op jit(solution)/shard_map/ppermute | solution.py:23
  14.5 1.2 convolution_bitcast_fusion
  15.7 3.5 %fusion.29 = f32[8,16,16,512]{3,2,1,0:T(8,128)S(1)} fusion(f32[8,16,16,128]{3,2,1,0:T(8,128)S(1)} %convolution_bitcast_fusion, f32[128]{0:T(128)S(1)} %iota_convert_fusion, f32[512]{0:T(512)S(1)} %multiply_add_fusion), kind=kOutput, calls=%fused_computation.67 | convolution fusion | flops 1610874880 | bytes 5245440 | tf_op jit(solution)/shard_map/mlib,jb->mlij/dot_general | solution.py:161
  21.6 17.7 %all-to-all-start = ((f32[16,2,1,16,512]{4,3,1,2,0:T(8,128)}), f32[16,2,1,16,512]{4,3,1,2,0:T(8,128)S(1)}, u32[]{:S(2)}, u32[]{:S(2)}) async-start(f32[16,2,1,16,512]{4,3,1,2,0:T(8,128)} %copy.26), calls=%async_computation | async-start | bytes 2097152 | tf_op jit(solution)/shard_map/all_to_all | solution.py:36
  39.4 49.8 %all-to-all-done = f32[16,2,1,16,512]{4,3,1,2,0:T(8,128)S(1)} async-done(((f32[16,2,1,16,512]{4,3,1,2,0:T(8,128)}), f32[16,2,1,16,512]{4,3,1,2,0:T(8,128)S(1)}, u32[]{:S(2)}, u32[]{:S(2)}) %all-to-all-start) | async-done | bytes 1048608 | tf_op jit(solution)/shard_map/all_to_all | solution.py:36
  89.2 4.3 %collective-permute-start.2 = (f32[2,1,1,512]{3,2,1,0:T(1,128)S(1)}, f32[2,1,1,512]{3,2,1,0:T(1,128)S(1)}, u32[]{:S(2)}, u32[]{:S(2)}) collective-permute-start(f32[2,1,1,512]{3,2,1,0:T(1,128)S(1)} %get-tuple-element.64), channel_id=1, source_target_pairs={{0,1},{1,2},{2,3},{3,4},{4,5},{5,6},{6,7},{7,8},{8,9},{9,10},{10,1... | collective-permute-start | bytes 12296 | tf_op jit(solution)/shard_map/ppermute | solution.py:22
  93.5 1.9 collective-permute-start.3
  95.5 5.6 %collective-permute-done.3 = f32[2,1,1,512]{3,2,1,0:T(1,128)S(1)} collective-permute-done((f32[2,1,1,512]{3,2,1,0:T(1,128)S(1)}, f32[2,1,1,512]{3,2,1,0:T(1,128)S(1)}, u32[]{:S(2)}, u32[]{:S(2)}) %collective-permute-start.3) | collective-permute-done | bytes 4128 | tf_op jit(solution)/shard_map/ppermute | solution.py:23
  101.4 1.3 select_reduce_fusion
  102.8 1.5 fusion.2
  104.3 2.0 collective-permute-start.4
  106.2 2.4 %collective-permute-start.5 = (f32[3,1,1,512]{3,2,1,0:T(1,128)S(1)}, f32[3,1,1,512]{3,2,1,0:T(1,128)S(1)}, u32[]{:S(2)}, u32[]{:S(2)}) collective-permute-start(f32[3,1,1,512]{3,2,1,0:T(1,128)S(1)} %get-tuple-element.63), channel_id=1, source_target_pairs={{1,0},{2,1},{3,2},{4,3},{5,4},{6,5},{7,6},{8,7},{9,8},{10,9},{11,1... | collective-permute-start | bytes 18440 | tf_op jit(solution)/shard_map/ppermute | solution.py:23
  108.6 5.3 %collective-permute-done.5 = f32[3,1,1,512]{3,2,1,0:T(1,128)S(1)} collective-permute-done((f32[3,1,1,512]{3,2,1,0:T(1,128)S(1)}, f32[3,1,1,512]{3,2,1,0:T(1,128)S(1)}, u32[]{:S(2)}, u32[]{:S(2)}) %collective-permute-start.5) | collective-permute-done | bytes 6176 | tf_op jit(solution)/shard_map/ppermute | solution.py:23
  114.4 56.8 %all_to_all.10 = f32[16,2,1,16,512]{4,3,1,2,0:T(8,128)S(1)} all-to-all(f32[16,2,1,16,512]{4,3,1,2,0:T(8,128)S(1)} %broadcast_in_dim.73), channel_id=1, replica_groups=mesh['mem'=16,'reg'=32] {'mem'}, dimensions={0} | all-to-all | bytes 2097152 | tf_op jit(solution)/shard_map/all_to_all | solution.py:42
  172.4 3.6 %fusion.27 = f32[8,16,16,128]{3,2,1,0:T(8,128)S(1)} fusion(f32[8,16,16,512]{3,2,1,0:T(8,128)S(1)} %fusion.1, f32[128]{0:T(128)S(1)} %iota_convert_fusion, f32[512]{0:T(512)S(1)} %multiply_add_fusion), kind=kOutput, calls=%fused_computation.65 | convolution fusion | flops 1610874880 | bytes 5245440 | tf_op jit(solution)/shard_map/mlij,jb->mlib/dot_general | solution.py:176
  176.8 2.3 %collective-permute-start.6 = (f32[8,16,128]{2,1,0:T(8,128)S(1)}, f32[8,16,128]{2,1,0:T(8,128)S(1)}, u32[]{:S(2)}, u32[]{:S(2)}) collective-permute-start(f32[8,16,128]{2,1,0:T(8,128)S(1)} %bitcast.104), channel_id=1, source_target_pairs={{1,0},{2,1},{3,2},{4,3},{5,4},{6,5},{7,6},{8,7},{9,8},{10,9},{11,1... | collective-permute-start | bytes 196616 | tf_op jit(solution)/shard_map/ppermute | solution.py:61
  179.2 6.0 %collective-permute-start.7 = (f32[8,16,128]{2,1,0:T(8,128)S(1)}, f32[8,16,128]{2,1,0:T(8,128)S(1)}, u32[]{:S(2)}, u32[]{:S(2)}) collective-permute-start(f32[8,16,128]{2,1,0:T(8,128)S(1)} %bitcast.103), channel_id=1, source_target_pairs={{0,1},{1,2},{2,3},{3,4},{4,5},{5,6},{6,7},{7,8},{8,9},{9,10},{10,1... | collective-permute-start | bytes 196616 | tf_op jit(solution)/shard_map/ppermute | solution.py:61
  185.2 1.3 collective-permute-done.7
  186.5 7.0 %collective-permute-start.8 = (f32[8,16,2,128]{3,1,0,2:T(8,128)S(1)}, f32[8,16,2,128]{3,1,0,2:T(8,128)S(1)}, u32[]{:S(2)}, u32[]{:S(2)}) collective-permute-start(f32[8,16,2,128]{3,1,0,2:T(8,128)S(1)} %get-tuple-element.48), channel_id=1, source_target_pairs={{0,1},{1,2},{2,3},{3,4},{4,5},{5,6},{6,7},{7,8},{8,9},{9,10},{10,1... | collective-permute-start | bytes 393224 | tf_op jit(solution)/shard_map/ppermute | solution.py:22
  193.6 1.9 collective-permute-start.9
  195.5 7.0 %collective-permute-done.9 = f32[8,16,2,128]{3,1,0,2:T(8,128)S(1)} collective-permute-done((f32[8,16,2,128]{3,1,0,2:T(8,128)S(1)}, f32[8,16,2,128]{3,1,0,2:T(8,128)S(1)}, u32[]{:S(2)}, u32[]{:S(2)}) %collective-permute-start.9) | collective-permute-done | bytes 131104 | tf_op jit(solution)/shard_map/ppermute | solution.py:23
  (67 shorter events, 8.8 us)
Async XLA Ops:
  0.0 6.1 %copy-start.2 = (f32[8,16,4,128]{3,2,1,0:T(4,128)S(1)}, f32[8,16,4,128]{3,2,1,0:T(4,128)}, u32[]{:S(2)}) copy-start(f32[8,16,4,128]{3,2,1,0:T(4,128)} %param.10) | copy-start | bytes 786436
  1.2 4.9 %collective-permute-start = (f32[8,16,3,128]{3,1,0,2:T(8,128)S(1)}, f32[8,16,3,128]{3,1,0,2:T(8,128)S(1)}, u32[]{:S(2)}, u32[]{:S(2)}) collective-permute-start(f32[8,16,3,128]{3,1,0,2:T(8,128)S(1)} %copy.40), channel_id=1, source_target_pairs={{0,1},{1,2},{2,3},{3,4},{4,5},{5,6},{6,7},{7,8},{8,9},{9,10},{10,1... | collective-permute-start | bytes 589832 | tf_op jit(solution)/shard_map/ppermute | solution.py:22
  3.6 9.7 %collective-permute-start.1 = (f32[8,16,3,128]{3,1,0,2:T(8,128)S(1)}, f32[8,16,3,128]{3,1,0,2:T(8,128)S(1)}, u32[]{:S(2)}, u32[]{:S(2)}) collective-permute-start(f32[8,16,3,128]{3,1,0,2:T(8,128)S(1)} %copy.41), channel_id=1, source_target_pairs={{1,0},{2,1},{3,2},{4,3},{5,4},{6,5},{7,6},{8,7},{9,8},{10,9},{11,1... | collective-permute-start | bytes 589832 | tf_op jit(solution)/shard_map/ppermute | solution.py:23
  15.7 3.5 %copy-start = (bf16[8,2,16,16,512]{4,3,2,1,0:T(8,128)(2,1)S(1)}, bf16[8,2,16,16,512]{4,3,2,1,0:T(8,128)(2,1)}, u32[]{:S(2)}) copy-start(bf16[8,2,16,16,512]{4,3,2,1,0:T(8,128)(2,1)} %param.11) | copy-start | bytes 12582916
  21.6 73.8 %copy-start.3 = (s32[1024]{0:T(1024)S(1)}, s32[1024]{0:T(1024)}, u32[]{:S(2)}) copy-start(s32[1024]{0:T(1024)} %param.12) | copy-start | bytes 12292
  21.6 73.8 %copy-start.4 = (s32[1024]{0:T(1024)S(1)}, s32[1024]{0:T(1024)}, u32[]{:S(2)}) copy-start(s32[1024]{0:T(1024)} %param.13) | copy-start | bytes 12292
  21.6 67.5 %all-to-all-start = ((f32[16,2,1,16,512]{4,3,1,2,0:T(8,128)}), f32[16,2,1,16,512]{4,3,1,2,0:T(8,128)S(1)}, u32[]{:S(2)}, u32[]{:S(2)}) async-start(f32[16,2,1,16,512]{4,3,1,2,0:T(8,128)} %copy.26), calls=%async_computation | async-start | bytes 2097152 | tf_op jit(solution)/shard_map/all_to_all | solution.py:36
  39.3 63.4 %copy-start.5 = (f32[1024]{0:T(1024)S(1)}, f32[1024]{0:T(1024)}, u32[]{:S(2)}) copy-start(f32[1024]{0:T(1024)} %param.15) | copy-start | bytes 12292
  39.4 63.4 %copy-start.6 = (f32[1024]{0:T(1024)S(1)}, f32[1024]{0:T(1024)}, u32[]{:S(2)}) copy-start(f32[1024]{0:T(1024)} %param.14) | copy-start | bytes 12292
  89.2 6.3 %collective-permute-start.2 = (f32[2,1,1,512]{3,2,1,0:T(1,128)S(1)}, f32[2,1,1,512]{3,2,1,0:T(1,128)S(1)}, u32[]{:S(2)}, u32[]{:S(2)}) collective-permute-start(f32[2,1,1,512]{3,2,1,0:T(1,128)S(1)} %get-tuple-element.64), channel_id=1, source_target_pairs={{0,1},{1,2},{2,3},{3,4},{4,5},{5,6},{6,7},{7,8},{8,9},{9,10},{10,1... | collective-permute-start | bytes 12296 | tf_op jit(solution)/shard_map/ppermute | solution.py:22
  93.5 7.6 %collective-permute-start.3 = (f32[2,1,1,512]{3,2,1,0:T(1,128)S(1)}, f32[2,1,1,512]{3,2,1,0:T(1,128)S(1)}, u32[]{:S(2)}, u32[]{:S(2)}) collective-permute-start(f32[2,1,1,512]{3,2,1,0:T(1,128)S(1)} %get-tuple-element.65), channel_id=1, source_target_pairs={{1,0},{2,1},{3,2},{4,3},{5,4},{6,5},{7,6},{8,7},{9,8},{10,9},{11,1... | collective-permute-start | bytes 12296 | tf_op jit(solution)/shard_map/ppermute | solution.py:23
  104.3 4.3 %collective-permute-start.4 = (f32[3,1,1,512]{3,2,1,0:T(1,128)S(1)}, f32[3,1,1,512]{3,2,1,0:T(1,128)S(1)}, u32[]{:S(2)}, u32[]{:S(2)}) collective-permute-start(f32[3,1,1,512]{3,2,1,0:T(1,128)S(1)} %get-tuple-element.62), channel_id=1, source_target_pairs={{0,1},{1,2},{2,3},{3,4},{4,5},{5,6},{6,7},{7,8},{8,9},{9,10},{10,1... | collective-permute-start | bytes 18440 | tf_op jit(solution)/shard_map/ppermute | solution.py:22
  106.2 7.6 %collective-permute-start.5 = (f32[3,1,1,512]{3,2,1,0:T(1,128)S(1)}, f32[3,1,1,512]{3,2,1,0:T(1,128)S(1)}, u32[]{:S(2)}, u32[]{:S(2)}) collective-permute-start(f32[3,1,1,512]{3,2,1,0:T(1,128)S(1)} %get-tuple-element.63), channel_id=1, source_target_pairs={{1,0},{2,1},{3,2},{4,3},{5,4},{6,5},{7,6},{8,7},{9,8},{10,9},{11,1... | collective-permute-start | bytes 18440 | tf_op jit(solution)/shard_map/ppermute | solution.py:23
  114.0 57.1 %copy-start.1 = (bf16[8,2,16,16,512]{4,3,2,1,0:T(8,128)(2,1)S(1)}, bf16[8,2,16,16,512]{4,3,2,1,0:T(8,128)(2,1)}, u32[]{:S(2)}) copy-start(bf16[8,2,16,16,512]{4,3,2,1,0:T(8,128)(2,1)} %param.11) | copy-start | bytes 12582916
  176.8 8.4 %collective-permute-start.6 = (f32[8,16,128]{2,1,0:T(8,128)S(1)}, f32[8,16,128]{2,1,0:T(8,128)S(1)}, u32[]{:S(2)}, u32[]{:S(2)}) collective-permute-start(f32[8,16,128]{2,1,0:T(8,128)S(1)} %bitcast.104), channel_id=1, source_target_pairs={{1,0},{2,1},{3,2},{4,3},{5,4},{6,5},{7,6},{8,7},{9,8},{10,9},{11,1... | collective-permute-start | bytes 196616 | tf_op jit(solution)/shard_map/ppermute | solution.py:61
  179.2 7.3 %collective-permute-start.7 = (f32[8,16,128]{2,1,0:T(8,128)S(1)}, f32[8,16,128]{2,1,0:T(8,128)S(1)}, u32[]{:S(2)}, u32[]{:S(2)}) collective-permute-start(f32[8,16,128]{2,1,0:T(8,128)S(1)} %bitcast.103), channel_id=1, source_target_pairs={{0,1},{1,2},{2,3},{3,4},{4,5},{5,6},{6,7},{7,8},{8,9},{9,10},{10,1... | collective-permute-start | bytes 196616 | tf_op jit(solution)/shard_map/ppermute | solution.py:61
  186.5 8.9 %collective-permute-start.8 = (f32[8,16,2,128]{3,1,0,2:T(8,128)S(1)}, f32[8,16,2,128]{3,1,0,2:T(8,128)S(1)}, u32[]{:S(2)}, u32[]{:S(2)}) collective-permute-start(f32[8,16,2,128]{3,1,0,2:T(8,128)S(1)} %get-tuple-element.48), channel_id=1, source_target_pairs={{0,1},{1,2},{2,3},{3,4},{4,5},{5,6},{6,7},{7,8},{8,9},{9,10},{10,1... | collective-permute-start | bytes 393224 | tf_op jit(solution)/shard_map/ppermute | solution.py:22
  193.6 9.0 %collective-permute-start.9 = (f32[8,16,2,128]{3,1,0,2:T(8,128)S(1)}, f32[8,16,2,128]{3,1,0,2:T(8,128)S(1)}, u32[]{:S(2)}, u32[]{:S(2)}) collective-permute-start(f32[8,16,2,128]{3,1,0,2:T(8,128)S(1)} %get-tuple-element.49), channel_id=1, source_target_pairs={{1,0},{2,1},{3,2},{4,3},{5,4},{6,5},{7,6},{8,7},{9,8},{10,9},{11,1... | collective-permute-start | bytes 393224 | tf_op jit(solution)/shard_map/ppermute | solution.py:23
where the time goes:
time: 205 us; the launch traced here: 204 us
  waiting for transfers between devices  76.3 us (37%)
  blocking collectives  56.8 us (28%)
  starting transfers between devices  49.9 us (24%)
  matrix products  11.8 us (6%)
  local copies, waits for them, and re-layouts  5.1 us (2%)
  other arithmetic  3.93 us (2%)
    all_to_all x1, blocking collectives, from_everyone(): lax.all_to_all(jnp.broadcast_to(value[None], (devices, *value.shape)), ax...  56.8 us
    all_to_all x1, waiting for transfers between devices, sum_at_owner(): lax.all_to_all(cut_along(value, dim, devices), axis, 0, 0, tiled=True)  49.8 us
    ppermute x4, waiting for transfers between devices, padded_2(): after = lax.ppermute(first, axis, down)  25 us
    all_to_all x1, starting transfers between devices, sum_at_owner(): lax.all_to_all(cut_along(value, dim, devices), axis, 0, 0, tiled=True)  17.7 us
    ppermute x4, starting transfers between devices, padded_2(): before = lax.ppermute(last, axis, up)  15.6 us
    ppermute x4, starting transfers between devices, padded_2(): after = lax.ppermute(first, axis, down)  8.41 us
    ppermute x2, starting transfers between devices, from_behind(): return lax.ppermute(value, axis, pairs)  8.26 us
  transfers between devices with their start and end apart: 11, of which 7 were waited for; matrix products, arithmetic and copies ran while one was open for 0% of the time, Pallas kernels for 0%

commit v1 on v0

v1 whole, which is shorter than its diff:
```python
import functools
import math

import jax
import jax.numpy as jnp
from jax import lax
from jax.experimental import pallas as pl
from jax.experimental.pallas import tpu as pltpu
from jax.sharding import PartitionSpec as P

MESH = pl.DeviceIdType.MESH
F32, BF16, I32 = jnp.float32, jnp.bfloat16, jnp.int32
diffuse = 0.2

YS = 4
ZS = 4
M, L, R, C = 8, 16, 4, 128
RX, NY, OBS = 16, 512, 1024
LINES = L * RX
NT = (((1,), (1,)), ((), ()))


def split(value):
    high = value.astype(BF16)
    return high, (value - high.astype(F32)).astype(BF16)


def dot(a, b):
    return jnp.dot(a, b, preferred_element_type=F32)


def dot_nt(a, b):
    return lax.dot_general(a, b, NT, preferred_element_type=F32)


def sides(value):
    lane = lax.broadcasted_iota(I32, value.shape, 1)
    left = jnp.where(lane == 0, 0.0, pltpu.roll(value, 1, 1))
    right = jnp.where(lane == C - 1, 0.0, pltpu.roll(value, C - 1, 1))
    return left + right


def one_pass(rows, first, last, inside):
    out = {}
    for k in range(first, last + 1):
        here, above, below = rows.get(k), rows.get(k - 1), rows.get(k + 1)
        vertical = [v for v in (above, below) if v is not None]
        beside = vertical[0] if len(vertical) == 1 else vertical[0] + vertical[1] if vertical else None
        if here is not None:
            beside = sides(here) if beside is None else beside + sides(here)
            value = here + diffuse * (beside - 4.0 * here)
        else:
            value = diffuse * beside
        out[k] = inside(k, value)
    return out


def kernel(
    scale,
    regions,
    alpha_hbm,
    pert_hbm,
    cell_ref,
    kind_ref,
    val_ref,
    wt_ref,
    out_ref,
    pert,
    alpha,
    slab,
    part,
    c0t,
    c1t,
    r0f,
    r1f,
    r0b,
    r1b,
    py2,
    pyt,
    thi,
    tlo,
    etop,
    ebot,
    rtop,
    rbot,
    ysend,
    yrecv,
    zsend,
    zrecv,
    zfar,
    lc,
    lh,
    ftop,
    fbot,
    gtop,
    gbot,
    grad,
    own,
    sup,
    sdn,
    qup,
    qdn,
    local_sem,
    send_sem,
    recv_sem,
):
    mem = lax.axis_index("mem")
    reg = lax.axis_index("reg")
    y, zh = lax.rem(mem, YS), mem // YS
    up = lax.rem(reg + 1, regions)
    down = lax.rem(reg + regions - 1, regions)
    has_prev = reg > 0
    has_next = reg < regions - 1
    y_peers = [zh * YS + lax.rem(y + d, YS) for d in range(1, YS)]
    z_up = lax.rem(zh + 1, ZS) * YS + y
    z_down = lax.rem(zh + ZS - 1, ZS) * YS + y

    def send(source, target, index, **where):
        copy = pltpu.make_async_remote_copy(
            src_ref=source,
            dst_ref=target,
            send_sem=send_sem.at[index],
            recv_sem=recv_sem.at[index],
            device_id=where,
            device_id_type=MESH,
        )
        copy.start()
        return copy

    barrier = pltpu.get_barrier_semaphore()
    for who in (up, down):
        pl.semaphore_signal(barrier, inc=1, device_id={"reg": who}, device_id_type=MESH)
    for who in y_peers + [z_up, z_down]:
        pl.semaphore_signal(barrier, inc=1, device_id={"mem": who}, device_id_type=MESH)
    get_alpha = pltpu.make_async_copy(alpha_hbm, alpha, local_sem.at[0])
    get_alpha.start()
    get_pert = pltpu.make_async_copy(pert_hbm, pert, local_sem.at[1])
    get_pert.start()
    get_alpha.wait()
    for r in range(R):
        slab[3 + r] = alpha[pl.ds(r, M * L, stride=R), :]
    pl.semaphore_wait(barrier, 2 + YS - 1 + 2)

    halo_up = send(slab.at[pl.ds(4, 3)], slab.at[pl.ds(0, 3)], 0, reg=up)
    halo_down = send(slab.at[pl.ds(3, 3)], slab.at[pl.ds(7, 3)], 1, reg=down)

    cell = cell_ref[...]
    kind = kind_ref[...]
    column = cell & (NY - 1)
    row_in = (cell >> 9) & (RX - 1)
    level = cell >> 13
    line = cell >> 9
    line_m = jnp.where(row_in > 0, line - 1, LINES + level)
    line_p = jnp.where(row_in < RX - 1, line + 1, LINES + L + level)

    def build_columns(step, _):
        at = pl.multiple_of(step * 32, 32)
        number = lax.broadcasted_iota(I32, (32, OBS), 0) + at
        c0t[pl.ds(at, 32), :] = jnp.where(number == column, 1.0, 0.0).astype(BF16)
        c1t[pl.ds(at, 32), :] = jnp.where(
            number == column + 1, 0.5, jnp.where(number == column - 1, -0.5, 0.0)
        ).astype(BF16)
        return _

    lax.fori_loop(0, NY // 32, build_columns, 0)

    def build_lines(step, _):
        at = pl.multiple_of(step * 32, 32)
        number = lax.broadcasted_iota(I32, (32, OBS), 0) + at
        r0 = jnp.where(number == line, 1.0, 0.0)
        r1 = jnp.where(number == line_p, 0.5, jnp.where(number == line_m, -0.5, 0.0))
        r0f[pl.ds(at, 32), :] = r0
        r1f[pl.ds(at, 32), :] = r1
        r0b[pl.ds(at, 32), :] = r0.astype(BF16)
        r1b[pl.ds(at, 32), :] = r1.astype(BF16)
        return _

    lax.fori_loop(0, (LINES + 2 * L) // 32, build_lines, 0)

    def table(shape, fine_dim):
        fine = lax.broadcasted_iota(I32, shape, fine_dim).astype(F32)
        coarse = lax.broadcasted_iota(I32, shape, 1 - fine_dim).astype(F32)
        return jnp.maximum(0.0, 1.0 - jnp.abs((fine + 0.5) / 4.0 - 0.5 - coarse)).astype(BF16)

    weights = table((C, NY), 1)
    py2[0:C, :] = weights
    py2[C : 2 * C, :] = weights
    pyt[...] = table((NY, C), 0)

    def inside(k, value):
        if k < 0:
            return jnp.where(has_prev, value, 0.0)
        if k >= R:
            return jnp.where(has_next, value, 0.0)
        return value

    halo_up.wait()
    halo_down.wait()

    def smooth_member(m, _):
        at = pl.multiple_of(m * L, L)
        rows = {k - 3: inside(k - 3, slab[k, pl.ds(at, L), :]) for k in range(R + 6)}
        rows = one_pass(rows, -2, R + 1, inside)
        rows = one_pass(rows, -1, R, inside)
        for i in range(RX):
            q, s = divmod(i, 4)
            mine, other = ((0.625, 0.375), (0.875, 0.125), (0.875, 0.125), (0.625, 0.375))[s]
            near = q - 1 if s < 2 else q + 1
            value = mine * rows[q] + other * rows[near]
            part[pl.ds(m * (L * RX) + i, L, stride=RX), :] = value
        return _

    lax.fori_loop(0, M, smooth_member, 0)
    get_pert.wait()

    LB = 2

    def increments(step, _):
        pieces = []
        for k in range(LB):
            for m in range(M):
                at = pl.multiple_of(m * (L * RX) + (step * LB + k) * RX, RX)
                pieces.append(part[pl.ds(at, RX), :])
        high, low = split(jnp.concatenate(pieces, axis=0))
        fine = dot(jnp.concatenate([high, low], axis=1), py2[...])
        for k in range(LB):
            lev = step * LB + k
            for w in range(2):
                total = None
                for m in range(M):
                    at = (k * M + m) * RX
                    term = fine[at : at + RX] * pert[m, w, lev].astype(F32)
                    total = term if total is None else total + term
                at = pl.multiple_of(w * LINES + lev * RX, RX)
                thi[pl.ds(at, RX), :], tlo[pl.ds(at, RX), :] = split(total)
                etop[w, pl.ds(lev, 1), :] = total[0:1]
                ebot[w, pl.ds(lev, 1), :] = total[RX - 1 : RX]
        return _

    lax.fori_loop(0, L // LB, increments, 0)

    edge_down = send(etop, rbot, 2, reg=down)
    edge_up = send(ebot, rtop, 3, reg=up)

    NB = 256

    def pick(step, _):
        at = pl.multiple_of(step * NB, NB)
        near, slope = c0t[:, pl.ds(at, NB)], c1t[:, pl.ds(at, NB)]
        second = kind_ref[:, pl.ds(at, NB)] == 2

        def picked(first, rhs):
            return dot(thi[first : first + LINES, :], rhs) + dot(tlo[first : first + LINES, :], rhs)

        on = r0f[0:LINES, pl.ds(at, NB)]
        at_u = picked(0, near)
        at_v = picked(LINES, near)
        ysend[0:1, pl.ds(at, NB)] = jnp.sum(on * at_u, axis=0, keepdims=True)
        ysend[1:2, pl.ds(at, NB)] = jnp.sum(on * at_v, axis=0, keepdims=True)
        ysend[2:3, pl.ds(at, NB)] = jnp.sum(
            r1f[0:LINES, pl.ds(at, NB)] * jnp.where(second, at_v, at_u), axis=0, keepdims=True
        )
        at_y = picked(0, slope)
        ysend[3:4, pl.ds(at, NB)] = jnp.sum(on * at_y, axis=0, keepdims=True)
        return _

    lax.fori_loop(0, OBS // NB, pick, 0)
    edge_down.wait()
    edge_up.wait()
    rims = []
    for w in range(2):
        rims.append(jnp.where(has_prev, rtop[w], 0.0))
        rims.append(jnp.where(has_next, rbot[w], 0.0))
    high, low = split(jnp.concatenate(rims, axis=0))
    rim = dot(high, c0t[...]) + dot(low, c0t[...])
    rim = jnp.where(kind == 2, rim[2 * L :], rim[: 2 * L])
    ysend[2:3, :] = ysend[2:3, :] + jnp.sum(r1f[LINES:, :] * rim, axis=0, keepdims=True)

    copies = [send(ysend, yrecv.at[d], 4 + d, mem=who) for d, who in enumerate(y_peers)]
    total = ysend[...]
    for d, copy in enumerate(copies):
        copy.wait()
        total = total + yrecv[d]
    zsend[...] = total
    near_up = send(zsend, zrecv.at[0], 8, mem=z_up)
    near_down = send(zsend, zrecv.at[1], 9, mem=z_down)
    near_up.wait()
    far_up = send(zrecv.at[0, pl.ds(0, 2)], zfar.at[pl.ds(0, 2)], 10, mem=z_up)
    near_down.wait()
    far_down = send(zrecv.at[1, pl.ds(2, 2)], zfar.at[pl.ds(2, 2)], 11, mem=z_down)
    total = total + zrecv[0] + zrecv[1]
    far_up.wait()
    far_down.wait()
    total = (total + zfar[...]) * scale

    u, v, slope_x, slope_y = total[0:1], total[1:2], total[2:3], total[3:4]
    is_u, is_v, is_vort, is_adv = kind == 0, kind == 1, kind == 2, kind == 3
    seen = jnp.where(
        is_u,
        u,
        jnp.where(is_v, v, jnp.where(is_vort, slope_x - slope_y, u * slope_x + v * slope_y)),
    )
    misfit = wt_ref[...] * (seen - val_ref[...]) * scale
    zero = jnp.zeros_like(misfit)
    to_u = split(jnp.where(is_u, misfit, jnp.where(is_adv, misfit * slope_x, zero)))
    to_v = split(jnp.where(is_v, misfit, jnp.where(is_adv, misfit * slope_y, zero)))
    along_u = split(jnp.where(is_adv, misfit * u, zero))
    along_v = split(jnp.where(is_vort, misfit, zero))
    across = split(jnp.where(is_vort, -misfit, jnp.where(is_adv, misfit * v, zero)))

    outer = r1b[LINES:, :]
    high = jnp.concatenate([outer * along_u[0], outer * along_v[0]], axis=0)
    low = jnp.concatenate([outer * along_u[1], outer * along_v[1]], axis=0)
    rim = dot_nt(high, c0t[...]) + dot_nt(low, c0t[...])
    for w in range(2):
        ftop[w] = rim[2 * w * L : (2 * w + 1) * L]
        fbot[w] = rim[(2 * w + 1) * L : (2 * w + 2) * L]
    back_down = send(ftop, gbot, 12, reg=down)
    back_up = send(fbot, gtop, 13, reg=up)

    for half in range(2):
        lc[half * LINES : (half + 1) * LINES, :] = (
            r0b[0:LINES, :] * to_u[half] + r1b[0:LINES, :] * along_u[half]
        )
        lc[(2 + half) * LINES : (3 + half) * LINES, :] = (
            r0b[0:LINES, :] * to_v[half] + r1b[0:LINES, :] * along_v[half]
        )
        lh[half * LINES : (half + 1) * LINES, :] = r0b[0:LINES, :] * across[half]

    def scatter(step, _):
        at = pl.multiple_of(step * NB, NB)
        near, slope = c0t[pl.ds(at, NB), :], c1t[pl.ds(at, NB), :]
        grad[0, :, pl.ds(at, NB)] = (
            dot_nt(lc[0:LINES, :], near)
            + dot_nt(lc[LINES : 2 * LINES, :], near)
            + dot_nt(lh[0:LINES, :], slope)
            + dot_nt(lh[LINES : 2 * LINES, :], slope)
        )
        grad[1, :, pl.ds(at, NB)] = dot_nt(lc[2 * LINES : 3 * LINES, :], near) + dot_nt(
            lc[3 * LINES : 4 * LINES, :], near
        )
        return _

    lax.fori_loop(0, NY // NB, scatter, 0)
    back_down.wait()
    back_up.wait()

    def project(step, _):
        pieces = []
        for k in range(LB):
            lev = step * LB + k
            at = pl.multiple_of(lev * RX, RX)
            row = lax.broadcasted_iota(I32, (RX, NY), 0)
            gradients = []
            for w in range(2):
                first = jnp.where(has_prev, gtop[w, pl.ds(lev, 1), :], 0.0)
                last = jnp.where(has_next, gbot[w, pl.ds(lev, 1), :], 0.0)
                gradients.append(
                    grad[w, pl.ds(at, RX), :]
                    + jnp.where(row == 0, first, jnp.where(row == RX - 1, last, 0.0))
                )
            for m in range(M):
                pieces.append(
                    gradients[0] * pert[m, 0, lev].astype(F32)
                    + gradients[1] * pert[m, 1, lev].astype(F32)
                )
        high, low = split(jnp.concatenate(pieces, axis=0))
        out = dot(high, pyt[...]) + dot(low, pyt[...])
        for k in range(LB):
            for m in range(M):
                at = pl.multiple_of(m * (L * RX) + (step * LB + k) * RX, RX)
                first = (k * M + m) * RX
                part[pl.ds(at, RX), :] = out[first : first + RX]
        return _

    lax.fori_loop(0, L // LB, project, 0)

    def spread_member(m, _):
        at = pl.multiple_of(m * L, L)
        f = [part[pl.ds(m * (L * RX) + i, L, stride=RX), :] for i in range(RX)]
        taps = (0.125, 0.375, 0.625, 0.875, 0.875, 0.625, 0.375, 0.125)
        rows = {}
        for q in range(-1, R + 1):
            value = None
            for t, tap in enumerate(taps):
                i = 4 * q - 2 + t
                if 0 <= i < RX:
                    term = tap * f[i]
                    value = term if value is None else value + term
            rows[q] = inside(q, value)
        rows = one_pass(rows, -2, R + 1, inside)
        rows = one_pass(rows, -3, R + 2, inside)
        for k in range(3):
            sdn[k, pl.ds(at, L), :] = rows[k - 3]
            sup[k, pl.ds(at, L), :] = rows[R + k]
        for k in range(R):
            own[k, pl.ds(at, L), :] = rows[k]
        return _

    lax.fori_loop(0, M, spread_member, 0)
    last_down = send(sdn, qdn, 14, reg=down)
    last_up = send(sup, qup, 15, reg=up)
    last_down.wait()
    last_up.wait()
    for r in range(R):
        value = own[r]
        if r < 3:
            value = value + jnp.where(has_prev, qup[r], 0.0)
        if r >= R - 3:
            value = value + jnp.where(has_next, qdn[r - (R - 3)], 0.0)
        out_ref[pl.ds(r, M * L, stride=R), :] = value


def local(regions, members, alpha, perturbation, obs_cell, obs_kind, obs_value, obs_weight):
    any_space = pl.BlockSpec(memory_space=pl.ANY)
    in_vmem = pl.BlockSpec(memory_space=pltpu.VMEM)
    row = (1, OBS)
    edge = pltpu.VMEM((2, L, NY), F32)
    rows3 = pltpu.VMEM((3, M * L, C), F32)
    out = pl.pallas_call(
        functools.partial(kernel, 1.0 / math.sqrt(members), regions),
        out_shape=jax.ShapeDtypeStruct((M * L * R, C), F32),
        in_specs=[any_space, any_space] + [in_vmem] * 4,
        out_specs=in_vmem,
        scratch_shapes=[
            pltpu.VMEM((M, 2, L, RX, NY), BF16),
            pltpu.VMEM((M * L * R, C), F32),
            pltpu.VMEM((R + 6, M * L, C), F32),
            pltpu.VMEM((M * L * RX, C), F32),
            pltpu.VMEM((NY, OBS), BF16),
            pltpu.VMEM((NY, OBS), BF16),
            pltpu.VMEM((LINES + 2 * L, OBS), F32),
            pltpu.VMEM((LINES + 2 * L, OBS), F32),
            pltpu.VMEM((LINES + 2 * L, OBS), BF16),
            pltpu.VMEM((LINES + 2 * L, OBS), BF16),
            pltpu.VMEM((2 * C, NY), BF16),
            pltpu.VMEM((NY, C), BF16),
            pltpu.VMEM((2 * LINES, NY), BF16),
            pltpu.VMEM((2 * LINES, NY), BF16),
            edge,
            edge,
            edge,
            edge,
            pltpu.VMEM((4, OBS), F32),
            pltpu.VMEM((YS - 1, 4, OBS), F32),
            pltpu.VMEM((4, OBS), F32),
            pltpu.VMEM((2, 4, OBS), F32),
            pltpu.VMEM((4, OBS), F32),
            pltpu.VMEM((4 * LINES, OBS), BF16),
            pltpu.VMEM((2 * LINES, OBS), BF16),
            edge,
            edge,
            edge,
            edge,
            pltpu.VMEM((2, LINES, NY), F32),
            pltpu.VMEM((R, M * L, C), F32),
            rows3,
            rows3,
            rows3,
            rows3,
            pltpu.SemaphoreType.DMA((2,)),
            pltpu.SemaphoreType.DMA((16,)),
            pltpu.SemaphoreType.DMA((16,)),
        ],
        compiler_params=pltpu.CompilerParams(
            collective_id=0, has_side_effects=True, vmem_limit_bytes=56 * 1024 * 1024
        ),
    )(
        alpha.reshape(M * L * R, C),
        perturbation,
        obs_cell.reshape(row),
        obs_kind.reshape(row),
        obs_value.reshape(row),
        obs_weight.reshape(row),
    )
    return out.reshape(M, L, R, C)


def solution(mesh):
    regions, groups = mesh.shape["reg"], mesh.shape["mem"]
    return jax.shard_map(
        functools.partial(local, regions, M * groups),
        mesh=mesh,
        in_specs=(
            P("mem", None, "reg", None),
            P("mem", None, None, "reg", None),
            P("reg"),
            P("reg"),
            P("reg"),
            P("reg"),
        ),
        out_specs=P("mem", None, "reg", None),
        check_vma=False,
    )
```

time: 205 us -> 61.3 us (0.30)
  the two profiles are of different devices: /device:TPU:99 before, /device:TPU:8 now
where the time goes in v1:
time: 61.3 us; the launch traced here: 61.1 us
  Pallas kernels  59.4 us (97%)
  local copies, waits for them, and re-layouts  1.67 us (3%)
    pallas_call x1, Pallas kernels, local(): pl.pallas_call(functools.partial(kernel, 1.0 / math.sqrt(members), region...  59.4 us
    unnamed x1, local copies, waits for them, and re-layouts  1.67 us

profile of v1, /device:TPU:8, one launch (start us, length us, event | category | flops | bytes accessed | tf_op | source)
XLA Modules:
  0.0 61.1 jit_solution(12792364460448592597)
XLA Ops:
  0.0 59.4 %shard_map.64 = f32[512,128]{1,0:T(8,128)} custom-call(f32[512,128]{1,0:T(8,128)} %bitcast.7, bf16[8,2,16,16,512]{4,3,2,1,0:T(8,128)(2,1)} %pert_hbm.1, s32[1,1024]{1,0:T(1,128)} %bitcast.8, s32[1,1024]{1,0:T(1,128)} %bitcast.9, f32[1,1024]{1,0:T(1,128)} %bitcast.10, f32[1,1024]{1,0:T(1,128)} %bitcast.11), custom_call_target="tpu_custom_call" | custom-call | tf_op jit(solution)/shard_map/pallas_call | solution.py:420
  59.4 1.7 %copy.8 = f32[8,16,4,128]{3,2,1,0:T(4,128)} copy(f32[8,16,4,128]{3,2,1,0:T(4,128)} %bitcast.6) | data formatting | bytes 524288

commit v2 on v1

v2 whole, which is shorter than its diff:
```python
import functools
import math

import jax
import jax.numpy as jnp
from jax import lax
from jax.experimental import pallas as pl
from jax.experimental.pallas import tpu as pltpu
from jax.sharding import PartitionSpec as P

MESH = pl.DeviceIdType.MESH
F32, BF16, I32 = jnp.float32, jnp.bfloat16, jnp.int32
diffuse = 0.2

YS = 4
ZS = 4
M, L, R, C = 8, 16, 4, 128
RX, NY, OBS = 16, 512, 1024
LINES = L * RX
LB = 2
CHUNKS = L // LB
ROWS = LB * M
GROUPS = 4
PER = CHUNKS // GROUPS
EDGE = 2 * (L // GROUPS)
NT = (((1,), (1,)), ((), ()))


def split(value):
    high = value.astype(BF16)
    return high, (value - high.astype(F32)).astype(BF16)


def dot(a, b):
    return jnp.dot(a, b, preferred_element_type=F32)


def dot_nt(a, b):
    return lax.dot_general(a, b, NT, preferred_element_type=F32)


def sides(value):
    lane = lax.broadcasted_iota(I32, value.shape, 1)
    left = jnp.where(lane == 0, 0.0, pltpu.roll(value, 1, 1))
    right = jnp.where(lane == C - 1, 0.0, pltpu.roll(value, C - 1, 1))
    return left + right


def one_pass(rows, first, last, inside):
    out = {}
    for k in range(first, last + 1):
        here, above, below = rows.get(k), rows.get(k - 1), rows.get(k + 1)
        vertical = [v for v in (above, below) if v is not None]
        beside = vertical[0] if len(vertical) == 1 else vertical[0] + vertical[1] if vertical else None
        if here is not None:
            beside = sides(here) if beside is None else beside + sides(here)
            value = here + diffuse * (beside - 4.0 * here)
        else:
            value = diffuse * beside
        out[k] = inside(k, value)
    return out


def kernel(
    scale,
    regions,
    alpha_hbm,
    pert_hbm,
    cell_ref,
    kind_ref,
    val_ref,
    wt_ref,
    out_ref,
    rest_ref,
    pert,
    alpha,
    slab,
    part,
    c0t,
    c1t,
    r0f,
    r1f,
    r0b,
    r1b,
    rimf,
    rimb,
    py2,
    pyt,
    thi,
    tlo,
    etop,
    ebot,
    rtop,
    rbot,
    ysend,
    yrecv,
    zsend,
    zrecv,
    zfar,
    lc,
    lh,
    ftop,
    fbot,
    gtop,
    gbot,
    grad,
    sup,
    sdn,
    qup,
    qdn,
    local_sem,
    send_sem,
    recv_sem,
):
    mem = lax.axis_index("mem")
    reg = lax.axis_index("reg")
    y, zh = lax.rem(mem, YS), mem // YS
    up = lax.rem(reg + 1, regions)
    down = lax.rem(reg + regions - 1, regions)
    has_prev = reg > 0
    has_next = reg < regions - 1
    y_peers = [zh * YS + lax.rem(y + d, YS) for d in range(1, YS)]
    z_up = lax.rem(zh + 1, ZS) * YS + y
    z_down = lax.rem(zh + ZS - 1, ZS) * YS + y

    def remote(source, target, index, **where):
        return pltpu.make_async_remote_copy(
            src_ref=source,
            dst_ref=target,
            send_sem=send_sem.at[index],
            recv_sem=recv_sem.at[index],
            device_id=where,
            device_id_type=MESH,
        )

    def send(*args, **where):
        copy = remote(*args, **where)
        copy.start()
        return copy

    def rims_in(c):
        at = pl.ds(pl.multiple_of(c * ROWS, ROWS), ROWS)
        return (
            remote(slab.at[pl.ds(4, 3), at], slab.at[pl.ds(0, 3), at], c, reg=up),
            remote(slab.at[pl.ds(3, 3), at], slab.at[pl.ds(7, 3), at], CHUNKS + c, reg=down),
        )

    def rims_out(c):
        at = pl.ds(pl.multiple_of(c * ROWS, ROWS), ROWS)
        first = 2 * CHUNKS
        return (
            remote(sdn.at[:, at], qdn.at[:, at], first + c, reg=down),
            remote(sup.at[:, at], qup.at[:, at], first + CHUNKS + c, reg=up),
        )

    def edges(g):
        first = 4 * CHUNKS
        return (
            remote(etop.at[g], rbot.at[g], first + g, reg=down),
            remote(ebot.at[g], rtop.at[g], first + GROUPS + g, reg=up),
        )

    def edges_back(g):
        first = 4 * CHUNKS + 2 * GROUPS
        return (
            remote(ftop.at[g], gbot.at[g], first + g, reg=down),
            remote(fbot.at[g], gtop.at[g], first + GROUPS + g, reg=up),
        )

    sums = 4 * CHUNKS + 4 * GROUPS

    def begin(copies):
        for copy in copies:
            copy.start()

    def finish(copies):
        for copy in copies:
            copy.wait()

    def each(count, body):
        def step(i, _):
            body(i)
            return _

        lax.fori_loop(0, count, step, 0)

    barrier = pltpu.get_barrier_semaphore()
    for who in (up, down):
        pl.semaphore_signal(barrier, inc=1, device_id={"reg": who}, device_id_type=MESH)
    for who in y_peers + [z_up, z_down]:
        pl.semaphore_signal(barrier, inc=1, device_id={"mem": who}, device_id_type=MESH)
    get_alpha = pltpu.make_async_copy(alpha_hbm, alpha, local_sem.at[0])
    get_alpha.start()
    get_pert = pltpu.make_async_copy(pert_hbm, pert, local_sem.at[1])
    get_pert.start()
    get_alpha.wait()

    def arrange(lev):
        at = pl.multiple_of(lev * M, M)
        for r in range(R):
            slab[3 + r, pl.ds(at, M), :] = alpha[pl.ds(lev * R + r, M, stride=L * R), :]

    each(L, arrange)
    pl.semaphore_wait(barrier, 2 + YS - 1 + 2)

    each(CHUNKS, lambda c: begin(rims_in(c)))

    cell = cell_ref[...]
    kind = kind_ref[...]
    column = cell & (NY - 1)
    row_in = (cell >> 9) & (RX - 1)
    level = cell >> 13
    line = cell >> 9
    line_m = jnp.where(row_in > 0, line - 1, -1)
    line_p = jnp.where(row_in < RX - 1, line + 1, -1)
    per = L // GROUPS
    place = (level // per) * EDGE + level % per + jnp.where(kind == 2, per, 0)
    place = jnp.where(row_in == 0, place, GROUPS * EDGE + place)
    place = jnp.where((kind >= 2) & ((row_in == 0) | (row_in == RX - 1)), place, -1)
    number = lax.broadcasted_iota(I32, (2 * GROUPS * EDGE, OBS), 0)
    outer = jnp.where(number == place, jnp.where(row_in == 0, -0.5, 0.5), 0.0)
    rimf[...] = outer
    rimb[...] = outer.astype(BF16)

    def build_columns(step, _):
        at = pl.multiple_of(step * 32, 32)
        number = lax.broadcasted_iota(I32, (32, OBS), 0) + at
        c0t[pl.ds(at, 32), :] = jnp.where(number == column, 1.0, 0.0).astype(BF16)
        c1t[pl.ds(at, 32), :] = jnp.where(
            number == column + 1, 0.5, jnp.where(number == column - 1, -0.5, 0.0)
        ).astype(BF16)
        return _

    lax.fori_loop(0, NY // 32, build_columns, 0)

    def build_lines(step, _):
        at = pl.multiple_of(step * 32, 32)
        number = lax.broadcasted_iota(I32, (32, OBS), 0) + at
        r0 = jnp.where(number == line, 1.0, 0.0)
        r1 = jnp.where(number == line_p, 0.5, jnp.where(number == line_m, -0.5, 0.0))
        r0f[pl.ds(at, 32), :] = r0
        r1f[pl.ds(at, 32), :] = r1
        r0b[pl.ds(at, 32), :] = r0.astype(BF16)
        r1b[pl.ds(at, 32), :] = r1.astype(BF16)
        return _

    lax.fori_loop(0, LINES // 32, build_lines, 0)

    def table(shape, fine_dim):
        fine = lax.broadcasted_iota(I32, shape, fine_dim).astype(F32)
        coarse = lax.broadcasted_iota(I32, shape, 1 - fine_dim).astype(F32)
        return jnp.maximum(0.0, 1.0 - jnp.abs((fine + 0.5) / 4.0 - 0.5 - coarse)).astype(BF16)

    weights = table((C, NY), 1)
    py2[0:C, :] = weights
    py2[C : 2 * C, :] = weights
    pyt[...] = table((NY, C), 0)

    def inside(k, value):
        if k < 0:
            return jnp.where(has_prev, value, 0.0)
        if k >= R:
            return jnp.where(has_next, value, 0.0)
        return value

    get_pert.wait()

    def increments(group):
        for h in range(PER):
            c = group * PER + h
            finish(rims_in(c))
            at = pl.multiple_of(c * ROWS, ROWS)
            rows = {k - 3: inside(k - 3, slab[k, pl.ds(at, ROWS), :]) for k in range(R + 6)}
            rows = one_pass(rows, -2, R + 1, inside)
            rows = one_pass(rows, -1, R, inside)
            at = pl.multiple_of(c * (ROWS * RX), ROWS * RX)
            for i in range(RX):
                q, s = divmod(i, 4)
                mine, other = ((0.625, 0.375), (0.875, 0.125), (0.875, 0.125), (0.625, 0.375))[s]
                near = q - 1 if s < 2 else q + 1
                part[pl.ds(at + i, ROWS, stride=RX), :] = mine * rows[q] + other * rows[near]
            high, low = split(part[pl.ds(at, ROWS * RX), :])
            fine = dot(jnp.concatenate([high, low], axis=1), py2[...])
            for k in range(LB):
                lev = c * LB + k
                for w in range(2):
                    total = None
                    for m in range(M):
                        at = (k * M + m) * RX
                        term = fine[at : at + RX] * pert[m, w, lev].astype(F32)
                        total = term if total is None else total + term
                    at = pl.multiple_of(w * LINES + lev * RX, RX)
                    thi[pl.ds(at, RX), :], tlo[pl.ds(at, RX), :] = split(total)
                    row = w * (EDGE // 2) + h * LB + k
                    etop[group, row : row + 1, :] = total[0:1]
                    ebot[group, row : row + 1, :] = total[RX - 1 : RX]
        begin(edges(group))

    each(GROUPS, increments)

    NB = 256

    def pick(step, _):
        at = pl.multiple_of(step * NB, NB)
        near, slope = c0t[:, pl.ds(at, NB)], c1t[:, pl.ds(at, NB)]
        second = kind_ref[:, pl.ds(at, NB)] == 2

        def picked(first, rhs):
            return dot(thi[first : first + LINES, :], rhs) + dot(tlo[first : first + LINES, :], rhs)

        on = r0f[0:LINES, pl.ds(at, NB)]
        at_u = picked(0, near)
        at_v = picked(LINES, near)
        ysend[0:1, pl.ds(at, NB)] = jnp.sum(on * at_u, axis=0, keepdims=True)
        ysend[1:2, pl.ds(at, NB)] = jnp.sum(on * at_v, axis=0, keepdims=True)
        ysend[2:3, pl.ds(at, NB)] = jnp.sum(
            r1f[0:LINES, pl.ds(at, NB)] * jnp.where(second, at_v, at_u), axis=0, keepdims=True
        )
        at_y = picked(0, slope)
        ysend[3:4, pl.ds(at, NB)] = jnp.sum(on * at_y, axis=0, keepdims=True)
        return _

    lax.fori_loop(0, OBS // NB, pick, 0)
    each(GROUPS, lambda g: finish(edges(g)))
    sides_in = [
        jnp.where(has_prev, rtop[...].reshape(GROUPS * EDGE, NY), 0.0),
        jnp.where(has_next, rbot[...].reshape(GROUPS * EDGE, NY), 0.0),
    ]
    high, low = split(jnp.concatenate(sides_in, axis=0))
    rim = dot(high, c0t[...]) + dot(low, c0t[...])
    ysend[2:3, :] = ysend[2:3, :] + jnp.sum(rimf[...] * rim, axis=0, keepdims=True)

    copies = [send(ysend, yrecv.at[d], sums + d, mem=who) for d, who in enumerate(y_peers)]
    total = ysend[...]
    for d, copy in enumerate(copies):
        copy.wait()
        total = total + yrecv[d]
    zsend[...] = total
    near_up = send(zsend, zrecv.at[0], sums + 3, mem=z_up)
    near_down = send(zsend, zrecv.at[1], sums + 4, mem=z_down)
    near_up.wait()
    far_up = send(zrecv.at[0, pl.ds(0, 2)], zfar.at[pl.ds(0, 2)], sums + 5, mem=z_up)
    near_down.wait()
    far_down = send(zrecv.at[1, pl.ds(2, 2)], zfar.at[pl.ds(2, 2)], sums + 6, mem=z_down)
    total = total + zrecv[0] + zrecv[1]
    far_up.wait()
    far_down.wait()
    total = (total + zfar[...]) * scale

    u, v, slope_x, slope_y = total[0:1], total[1:2], total[2:3], total[3:4]
    is_u, is_v, is_vort, is_adv = kind == 0, kind == 1, kind == 2, kind == 3
    seen = jnp.where(
        is_u,
        u,
        jnp.where(is_v, v, jnp.where(is_vort, slope_x - slope_y, u * slope_x + v * slope_y)),
    )
    misfit = wt_ref[...] * (seen - val_ref[...]) * scale
    zero = jnp.zeros_like(misfit)
    to_u = split(jnp.where(is_u, misfit, jnp.where(is_adv, misfit * slope_x, zero)))
    to_v = split(jnp.where(is_v, misfit, jnp.where(is_adv, misfit * slope_y, zero)))
    along_u = split(jnp.where(is_adv, misfit * u, zero))
    along_v = split(jnp.where(is_vort, misfit, zero))
    across = split(jnp.where(is_vort, -misfit, jnp.where(is_adv, misfit * v, zero)))

    high = rimb[...] * (along_u[0] + along_v[0])
    low = rimb[...] * (along_u[1] + along_v[1])
    rim = dot_nt(high, c0t[...]) + dot_nt(low, c0t[...])
    ftop[...] = rim[: GROUPS * EDGE].reshape(GROUPS, EDGE, NY)
    fbot[...] = rim[GROUPS * EDGE :].reshape(GROUPS, EDGE, NY)
    each(GROUPS, lambda g: begin(edges_back(g)))

    for half in range(2):
        lc[half * LINES : (half + 1) * LINES, :] = (
            r0b[0:LINES, :] * to_u[half] + r1b[0:LINES, :] * along_u[half]
        )
        lc[(2 + half) * LINES : (3 + half) * LINES, :] = (
            r0b[0:LINES, :] * to_v[half] + r1b[0:LINES, :] * along_v[half]
        )
        lh[half * LINES : (half + 1) * LINES, :] = r0b[0:LINES, :] * across[half]

    def scatter(step, _):
        at = pl.multiple_of(step * NB, NB)
        near, slope = c0t[pl.ds(at, NB), :], c1t[pl.ds(at, NB), :]
        grad[0, :, pl.ds(at, NB)] = (
            dot_nt(lc[0:LINES, :], near)
            + dot_nt(lc[LINES : 2 * LINES, :], near)
            + dot_nt(lh[0:LINES, :], slope)
            + dot_nt(lh[LINES : 2 * LINES, :], slope)
        )
        grad[1, :, pl.ds(at, NB)] = dot_nt(lc[2 * LINES : 3 * LINES, :], near) + dot_nt(
            lc[3 * LINES : 4 * LINES, :], near
        )
        return _

    lax.fori_loop(0, NY // NB, scatter, 0)

    def project(group):
        finish(edges_back(group))
        for h in range(PER):
            c = group * PER + h
            pieces = []
            row = lax.broadcasted_iota(I32, (RX, NY), 0)
            for k in range(LB):
                lev = c * LB + k
                at = pl.multiple_of(lev * RX, RX)
                gradients = []
                for w in range(2):
                    edge = w * (EDGE // 2) + h * LB + k
                    first = jnp.where(has_prev, gtop[group, edge : edge + 1, :], 0.0)
                    last = jnp.where(has_next, gbot[group, edge : edge + 1, :], 0.0)
                    gradients.append(
                        grad[w, pl.ds(at, RX), :]
                        + jnp.where(row == 0, first, jnp.where(row == RX - 1, last, 0.0))
                    )
                for m in range(M):
                    pieces.append(
                        gradients[0] * pert[m, 0, lev].astype(F32)
                        + gradients[1] * pert[m, 1, lev].astype(F32)
                    )
            high, low = split(jnp.concatenate(pieces, axis=0))
            at = pl.multiple_of(c * (ROWS * RX), ROWS * RX)
            part[pl.ds(at, ROWS * RX), :] = dot(high, pyt[...]) + dot(low, pyt[...])
            f = [part[pl.ds(at + i, ROWS, stride=RX), :] for i in range(RX)]
            taps = (0.125, 0.375, 0.625, 0.875, 0.875, 0.625, 0.375, 0.125)
            rows = {}
            for q in range(-1, R + 1):
                value = None
                for t, tap in enumerate(taps):
                    i = 4 * q - 2 + t
                    if 0 <= i < RX:
                        term = tap * f[i]
                        value = term if value is None else value + term
                rows[q] = inside(q, value)
            rows = one_pass(rows, -2, R + 1, inside)
            rows = one_pass(rows, -3, R + 2, inside)
            at = pl.multiple_of(c * ROWS, ROWS)
            for k in range(3):
                sdn[k, pl.ds(at, ROWS), :] = rows[k - 3]
                sup[k, pl.ds(at, ROWS), :] = rows[R + k]
            for k in range(LB):
                for r in range(R):
                    out_ref[pl.ds((c * LB + k) * R + r, M, stride=L * R), :] = rows[r][
                        k * M : (k + 1) * M
                    ]
            begin(rims_out(c))

    each(GROUPS, project)

    def collect(c):
        finish(rims_out(c))
        for k in range(LB):
            at = pl.multiple_of(c * ROWS + k * M, M)
            for r in range(R):
                value = 0.0
                if r < 3:
                    value = value + jnp.where(has_prev, qup[r, pl.ds(at, M), :], 0.0)
                if r >= R - 3:
                    value = value + jnp.where(has_next, qdn[r - (R - 3), pl.ds(at, M), :], 0.0)
                rest_ref[pl.ds((c * LB + k) * R + r, M, stride=L * R), :] = value

    each(CHUNKS, collect)


def local(regions, members, alpha, perturbation, obs_cell, obs_kind, obs_value, obs_weight):
    any_space = pl.BlockSpec(memory_space=pl.ANY)
    in_vmem = pl.BlockSpec(memory_space=pltpu.VMEM)
    row = (1, OBS)
    edge = pltpu.VMEM((GROUPS, EDGE, NY), F32)
    rows3 = pltpu.VMEM((3, M * L, C), F32)
    out, rest = pl.pallas_call(
        functools.partial(kernel, 1.0 / math.sqrt(members), regions),
        out_shape=[jax.ShapeDtypeStruct((M * L * R, C), F32)] * 2,
        in_specs=[any_space, any_space] + [in_vmem] * 4,
        out_specs=[in_vmem] * 2,
        scratch_shapes=[
            pltpu.VMEM((M, 2, L, RX, NY), BF16),
            pltpu.VMEM((M * L * R, C), F32),
            pltpu.VMEM((R + 6, M * L, C), F32),
            pltpu.VMEM((M * L * RX, C), F32),
            pltpu.VMEM((NY, OBS), BF16),
            pltpu.VMEM((NY, OBS), BF16),
            pltpu.VMEM((LINES, OBS), F32),
            pltpu.VMEM((LINES, OBS), F32),
            pltpu.VMEM((LINES, OBS), BF16),
            pltpu.VMEM((LINES, OBS), BF16),
            pltpu.VMEM((2 * GROUPS * EDGE, OBS), F32),
            pltpu.VMEM((2 * GROUPS * EDGE, OBS), BF16),
            pltpu.VMEM((2 * C, NY), BF16),
            pltpu.VMEM((NY, C), BF16),
            pltpu.VMEM((2 * LINES, NY), BF16),
            pltpu.VMEM((2 * LINES, NY), BF16),
            edge,
            edge,
            edge,
            edge,
            pltpu.VMEM((4, OBS), F32),
            pltpu.VMEM((YS - 1, 4, OBS), F32),
            pltpu.VMEM((4, OBS), F32),
            pltpu.VMEM((2, 4, OBS), F32),
            pltpu.VMEM((4, OBS), F32),
            pltpu.VMEM((4 * LINES, OBS), BF16),
            pltpu.VMEM((2 * LINES, OBS), BF16),
            edge,
            edge,
            edge,
            edge,
            pltpu.VMEM((2, LINES, NY), F32),
            rows3,
            rows3,
            rows3,
            rows3,
            pltpu.SemaphoreType.DMA((2,)),
            pltpu.SemaphoreType.DMA((4 * CHUNKS + 4 * GROUPS + YS + 3,)),
            pltpu.SemaphoreType.DMA((4 * CHUNKS + 4 * GROUPS + YS + 3,)),
        ],
        compiler_params=pltpu.CompilerParams(
            collective_id=0, has_side_effects=True, vmem_limit_bytes=56 * 1024 * 1024
        ),
    )(
        alpha.reshape(M * L * R, C),
        perturbation,
        obs_cell.reshape(row),
        obs_kind.reshape(row),
        obs_value.reshape(row),
        obs_weight.reshape(row),
    )
    return (out + rest).reshape(M, L, R, C)


def solution(mesh):
    regions, groups = mesh.shape["reg"], mesh.shape["mem"]
    return jax.shard_map(
        functools.partial(local, regions, M * groups),
        mesh=mesh,
        in_specs=(
            P("mem", None, "reg", None),
            P("mem", None, None, "reg", None),
            P("reg"),
            P("reg"),
            P("reg"),
            P("reg"),
        ),
        out_specs=P("mem", None, "reg", None),
        check_vma=False,
    )
```

time: 61.3 us -> 57.2 us (0.933)
  Pallas kernels: 59.4 us -> 55.3 us
  other arithmetic: 0 us -> 1.76 us
  local copies, waits for them, and re-layouts: 1.67 us -> 0 us
    pallas_call x1, Pallas kernels: 59.4 us -> 55.3 us  [local(): pl.pallas_call(functools.partial(kernel, 1.0 / math.sqrt(members), region...]
    add x0 -> x1, other arithmetic: none -> 1.76 us  [local(): return (out + rest).reshape(M, L, R, C)]
    unnamed x1 -> x0, local copies, waits for them, and re-layouts: 1.67 us -> none
where the time goes in v2:
time: 57.2 us; the launch traced here: 57.1 us
  Pallas kernels  55.3 us (97%)
  other arithmetic  1.76 us (3%)
    pallas_call x1, Pallas kernels, local(): pl.pallas_call(functools.partial(kernel, 1.0 / math.sqrt(members), region...  55.3 us
    add x1, other arithmetic, local(): return (out + rest).reshape(M, L, R, C)  1.76 us

profile of v2, /device:TPU:8, one launch (start us, length us, event | category | flops | bytes accessed | tf_op | source)
XLA Modules:
  0.0 57.1 jit_solution(12208186406981558110)
XLA Ops:
  0.0 55.3 %shard_map.64 = (f32[512,128]{1,0:T(8,128)}, f32[512,128]{1,0:T(8,128)}) custom-call(f32[512,128]{1,0:T(8,128)} %bitcast.6, bf16[8,2,16,16,512]{4,3,2,1,0:T(8,128)(2,1)} %pert_hbm.1, s32[1,1024]{1,0:T(1,128)} %bitcast.7, s32[1,1024]{1,0:T(1,128)} %bitcast.8, f32[1,1024]{1,0:T(1,128)} %bitcast.9, f32[1,1024]{1,0:T(1,128)} %bitcast.10), custom_call_target="tpu_custom_call" | custom-call | tf_op jit(solution)/shard_map/pallas_call | solution.py:470
  55.3 1.8 %add.3 = f32[512,128]{1,0:T(8,128)} add(f32[512,128]{1,0:T(8,128)} %get-tuple-element.7, f32[512,128]{1,0:T(8,128)} %get-tuple-element.8) | non-fusion elementwise | flops 65536 | bytes 786432 | tf_op jit(solution)/shard_map/add | solution.py:527

commit v3 on v2

--- a/solution.py
+++ b/solution.py
@@ -86,17 +86,12 @@
     rimb,
     py2,
     pyt,
-    thi,
-    tlo,
+    fields,
     etop,
     ebot,
     rtop,
     rbot,
-    ysend,
-    yrecv,
-    zsend,
-    zrecv,
-    zfar,
+    streams,
     lc,
     lh,
     ftop,
@@ -167,7 +162,47 @@
             remote(fbot.at[g], gtop.at[g], first + GROUPS + g, reg=up),
         )
 
+    winds, acrosses, alongs = streams
     sums = 4 * CHUNKS + 4 * GROUPS
+
+    def y_copies(n):
+        mine, from_y = streams[n][0], streams[n][1]
+        return [
+            remote(mine, from_y.at[d], sums + 6 * n + d, mem=who) for d, who in enumerate(y_peers)
+        ]
+
+    def near(n, turn):
+        held, from_z = streams[n][2], streams[n][3]
+        side = turn if n == 0 else 1 - turn
+        where = (z_up, z_down)[side]
+        return remote(held, from_z.at[side], sums + 6 * n + 3 + side, mem=where)
+
+    def far(n):
+        from_z, from_far = streams[n][3], streams[n][4]
+        where, side = (z_up, 0) if n == 0 else (z_down, 1)
+        return remote(from_z.at[side], from_far, sums + 6 * n + 5, mem=where)
+
+    def y_start(n):
+        begin(y_copies(n))
+
+    def y_end(n):
+        mine, from_y, held = streams[n][:3]
+        finish(y_copies(n))
+        total = mine[...]
+        for d in range(YS - 1):
+            total = total + from_y[d]
+        held[...] = total
+        begin((near(n, 0), near(n, 1)))
+
+    def z_middle(n):
+        near(n, 0).wait()
+        far(n).start()
+
+    def z_end(n):
+        held, from_z, from_far = streams[n][2:]
+        near(n, 1).wait()
+        far(n).wait()
+        return held[...] + from_z[0] + from_z[1] + from_far[...]
 
     def begin(copies):
         for copy in copies:
@@ -189,21 +224,26 @@
         pl.semaphore_signal(barrier, inc=1, device_id={"reg": who}, device_id_type=MESH)
     for who in y_peers + [z_up, z_down]:
         pl.semaphore_signal(barrier, inc=1, device_id={"mem": who}, device_id_type=MESH)
-    get_alpha = pltpu.make_async_copy(alpha_hbm, alpha, local_sem.at[0])
-    get_alpha.start()
-    get_pert = pltpu.make_async_copy(pert_hbm, pert, local_sem.at[1])
+    def get_alpha(c):
+        at = pl.ds(pl.multiple_of(c * (LB * R), LB * R), LB * R)
+        return pltpu.make_async_copy(alpha_hbm.at[:, at], alpha.at[:, at], local_sem.at[1 + c])
+
+    each(CHUNKS, lambda c: get_alpha(c).start())
+    get_pert = pltpu.make_async_copy(pert_hbm, pert, local_sem.at[0])
     get_pert.start()
-    get_alpha.wait()
-
-    def arrange(lev):
-        at = pl.multiple_of(lev * M, M)
-        for r in range(R):
-            slab[3 + r, pl.ds(at, M), :] = alpha[pl.ds(lev * R + r, M, stride=L * R), :]
-
-    each(L, arrange)
     pl.semaphore_wait(barrier, 2 + YS - 1 + 2)
-
-    each(CHUNKS, lambda c: begin(rims_in(c)))
+    flat = alpha.reshape(M * L * R, C)
+
+    def arrange(c):
+        get_alpha(c).wait()
+        for k in range(LB):
+            lev = c * LB + k
+            at = pl.multiple_of(lev * M, M)
+            for r in range(R):
+                slab[3 + r, pl.ds(at, M), :] = flat[pl.ds(lev * R + r, M, stride=L * R), :]
+        begin(rims_in(c))
+
+    each(CHUNKS, arrange)
 
     cell = cell_ref[...]
     kind = kind_ref[...]
@@ -289,8 +329,8 @@
                         at = (k * M + m) * RX
                         term = fine[at : at + RX] * pert[m, w, lev].astype(F32)
                         total = term if total is None else total + term
-                    at = pl.multiple_of(w * LINES + lev * RX, RX)
-                    thi[pl.ds(at, RX), :], tlo[pl.ds(at, RX), :] = split(total)
+                    at = pl.multiple_of(lev * RX, RX)
+                    fields[2 * w, pl.ds(at, RX), :], fields[2 * w + 1, pl.ds(at, RX), :] = split(total)
                     row = w * (EDGE // 2) + h * LB + k
                     etop[group, row : row + 1, :] = total[0:1]
                     ebot[group, row : row + 1, :] = total[RX - 1 : RX]
@@ -302,25 +342,26 @@
 
     def pick(step, _):
         at = pl.multiple_of(step * NB, NB)
-        near, slope = c0t[:, pl.ds(at, NB)], c1t[:, pl.ds(at, NB)]
-        second = kind_ref[:, pl.ds(at, NB)] == 2
-
-        def picked(first, rhs):
-            return dot(thi[first : first + LINES, :], rhs) + dot(tlo[first : first + LINES, :], rhs)
-
-        on = r0f[0:LINES, pl.ds(at, NB)]
-        at_u = picked(0, near)
-        at_v = picked(LINES, near)
-        ysend[0:1, pl.ds(at, NB)] = jnp.sum(on * at_u, axis=0, keepdims=True)
-        ysend[1:2, pl.ds(at, NB)] = jnp.sum(on * at_v, axis=0, keepdims=True)
-        ysend[2:3, pl.ds(at, NB)] = jnp.sum(
-            r1f[0:LINES, pl.ds(at, NB)] * jnp.where(second, at_v, at_u), axis=0, keepdims=True
-        )
-        at_y = picked(0, slope)
-        ysend[3:4, pl.ds(at, NB)] = jnp.sum(on * at_y, axis=0, keepdims=True)
+        at = pl.ds(at, NB)
+        second = kind_ref[:, at] == 2
+        on, beside = r0f[:, at], r1f[:, at]
+
+        def over(lines):
+            return jnp.sum(lines, axis=0, keepdims=True)
+
+        value = dot(fields[...].reshape(4 * LINES, NY), c0t[:, at])
+        at_u = value[0:LINES] + value[LINES : 2 * LINES]
+        at_v = value[2 * LINES : 3 * LINES] + value[3 * LINES :]
+        winds[0][0:1, at] = over(on * at_u)
+        winds[0][1:2, at] = over(on * at_v)
+        alongs[0][:, at] = over(beside * jnp.where(second, at_v, at_u))
+        value = dot(fields[0:2].reshape(2 * LINES, NY), c1t[:, at])
+        acrosses[0][:, at] = over(on * (value[0:LINES] + value[LINES:]))
         return _
 
     lax.fori_loop(0, OBS // NB, pick, 0)
+    y_start(0)
+    y_start(1)
     each(GROUPS, lambda g: finish(edges(g)))
     sides_in = [
         jnp.where(has_prev, rtop[...].reshape(GROUPS * EDGE, NY), 0.0),
@@ -328,26 +369,15 @@
     ]
     high, low = split(jnp.concatenate(sides_in, axis=0))
     rim = dot(high, c0t[...]) + dot(low, c0t[...])
-    ysend[2:3, :] = ysend[2:3, :] + jnp.sum(rimf[...] * rim, axis=0, keepdims=True)
-
-    copies = [send(ysend, yrecv.at[d], sums + d, mem=who) for d, who in enumerate(y_peers)]
-    total = ysend[...]
-    for d, copy in enumerate(copies):
-        copy.wait()
-        total = total + yrecv[d]
-    zsend[...] = total
-    near_up = send(zsend, zrecv.at[0], sums + 3, mem=z_up)
-    near_down = send(zsend, zrecv.at[1], sums + 4, mem=z_down)
-    near_up.wait()
-    far_up = send(zrecv.at[0, pl.ds(0, 2)], zfar.at[pl.ds(0, 2)], sums + 5, mem=z_up)
-    near_down.wait()
-    far_down = send(zrecv.at[1, pl.ds(2, 2)], zfar.at[pl.ds(2, 2)], sums + 6, mem=z_down)
-    total = total + zrecv[0] + zrecv[1]
-    far_up.wait()
-    far_down.wait()
-    total = (total + zfar[...]) * scale
-
-    u, v, slope_x, slope_y = total[0:1], total[1:2], total[2:3], total[3:4]
+    alongs[0][...] = alongs[0][...] + jnp.sum(rimf[...] * rim, axis=0, keepdims=True)
+    y_start(2)
+
+    for n in range(3):
+        y_end(n)
+    for n in range(3):
+        z_middle(n)
+    (both, slope_y, slope_x) = (z_end(n) * scale for n in range(3))
+    u, v = both[0:1], both[1:2]
     is_u, is_v, is_vort, is_adv = kind == 0, kind == 1, kind == 2, kind == 3
     seen = jnp.where(
         is_u,
@@ -380,16 +410,12 @@
 
     def scatter(step, _):
         at = pl.multiple_of(step * NB, NB)
-        near, slope = c0t[pl.ds(at, NB), :], c1t[pl.ds(at, NB), :]
-        grad[0, :, pl.ds(at, NB)] = (
-            dot_nt(lc[0:LINES, :], near)
-            + dot_nt(lc[LINES : 2 * LINES, :], near)
-            + dot_nt(lh[0:LINES, :], slope)
-            + dot_nt(lh[LINES : 2 * LINES, :], slope)
-        )
-        grad[1, :, pl.ds(at, NB)] = dot_nt(lc[2 * LINES : 3 * LINES, :], near) + dot_nt(
-            lc[3 * LINES : 4 * LINES, :], near
-        )
+        value = dot_nt(lc[...], c0t[pl.ds(at, NB), :])
+        slope = dot_nt(lh[...], c1t[pl.ds(at, NB), :])
+        grad[0, :, pl.ds(at, NB)] = (value[0:LINES] + value[LINES : 2 * LINES]) + (
+            slope[0:LINES] + slope[LINES:]
+        )
+        grad[1, :, pl.ds(at, NB)] = value[2 * LINES : 3 * LINES] + value[3 * LINES :]
         return _
 
     lax.fori_loop(0, NY // NB, scatter, 0)
@@ -419,7 +445,8 @@
                     )
             high, low = split(jnp.concatenate(pieces, axis=0))
             at = pl.multiple_of(c * (ROWS * RX), ROWS * RX)
-            part[pl.ds(at, ROWS * RX), :] = dot(high, pyt[...]) + dot(low, pyt[...])
+            value = dot(jnp.concatenate([high, low], axis=0), pyt[...])
+            part[pl.ds(at, ROWS * RX), :] = value[: ROWS * RX] + value[ROWS * RX :]
             f = [part[pl.ds(at + i, ROWS, stride=RX), :] for i in range(RX)]
             taps = (0.125, 0.375, 0.625, 0.875, 0.875, 0.625, 0.375, 0.125)
             rows = {}
@@ -467,6 +494,17 @@
     row = (1, OBS)
     edge = pltpu.VMEM((GROUPS, EDGE, NY), F32)
     rows3 = pltpu.VMEM((3, M * L, C), F32)
+
+    def stream(rows):
+        one = pltpu.VMEM((rows, OBS), F32)
+        return (
+            one,
+            pltpu.VMEM((YS - 1, rows, OBS), F32),
+            one,
+            pltpu.VMEM((2, rows, OBS), F32),
+            one,
+        )
+
     out, rest = pl.pallas_call(
         functools.partial(kernel, 1.0 / math.sqrt(members), regions),
         out_shape=[jax.ShapeDtypeStruct((M * L * R, C), F32)] * 2,
@@ -474,7 +512,7 @@
         out_specs=[in_vmem] * 2,
         scratch_shapes=[
             pltpu.VMEM((M, 2, L, RX, NY), BF16),
-            pltpu.VMEM((M * L * R, C), F32),
+            pltpu.VMEM((M, L * R, C), F32),
             pltpu.VMEM((R + 6, M * L, C), F32),
             pltpu.VMEM((M * L * RX, C), F32),
             pltpu.VMEM((NY, OBS), BF16),
@@ -487,17 +525,12 @@
             pltpu.VMEM((2 * GROUPS * EDGE, OBS), BF16),
             pltpu.VMEM((2 * C, NY), BF16),
             pltpu.VMEM((NY, C), BF16),
-            pltpu.VMEM((2 * LINES, NY), BF16),
-            pltpu.VMEM((2 * LINES, NY), BF16),
-            edge,
-            edge,
-            edge,
-            edge,
-            pltpu.VMEM((4, OBS), F32),
-            pltpu.VMEM((YS - 1, 4, OBS), F32),
-            pltpu.VMEM((4, OBS), F32),
-            pltpu.VMEM((2, 4, OBS), F32),
-            pltpu.VMEM((4, OBS), F32),
+            pltpu.VMEM((4, LINES, NY), BF16),
+            edge,
+            edge,
+            edge,
+            edge,
+            tuple(stream(rows) for rows in (2, 1, 1)),
             pltpu.VMEM((4 * LINES, OBS), BF16),
             pltpu.VMEM((2 * LINES, OBS), BF16),
             edge,
@@ -509,15 +542,15 @@
             rows3,
             rows3,
             rows3,
-            pltpu.SemaphoreType.DMA((2,)),
-            pltpu.SemaphoreType.DMA((4 * CHUNKS + 4 * GROUPS + YS + 3,)),
-            pltpu.SemaphoreType.DMA((4 * CHUNKS + 4 * GROUPS + YS + 3,)),
+            pltpu.SemaphoreType.DMA((1 + CHUNKS,)),
+            pltpu.SemaphoreType.DMA((4 * CHUNKS + 4 * GROUPS + 18,)),
+            pltpu.SemaphoreType.DMA((4 * CHUNKS + 4 * GROUPS + 18,)),
         ],
         compiler_params=pltpu.CompilerParams(
             collective_id=0, has_side_effects=True, vmem_limit_bytes=56 * 1024 * 1024
         ),
     )(
-        alpha.reshape(M * L * R, C),
+        alpha.reshape(M, L * R, C),
         perturbation,
         obs_cell.reshape(row),
         obs_kind.reshape(row),

time: 57.2 us -> 57.4 us (level)
  no operation moved by 1% of the time
where the time goes in v3:
time: 57.4 us; the launch traced here: 57.3 us
  Pallas kernels  55.5 us (97%)
  other arithmetic  1.76 us (3%)
    pallas_call x1, Pallas kernels, local(): pl.pallas_call(functools.partial(kernel, 1.0 / math.sqrt(members), region...  55.5 us
    add x1, other arithmetic, local(): return (out + rest).reshape(M, L, R, C)  1.76 us

profile of v3, /device:TPU:8, one launch (start us, length us, event | category | flops | bytes accessed | tf_op | source)
XLA Modules:
  0.0 57.3 jit_solution(2479601494874412885)
XLA Ops:
  0.0 55.5 %shard_map.64 = (f32[512,128]{1,0:T(8,128)}, f32[512,128]{1,0:T(8,128)}) custom-call(f32[8,64,128]{2,1,0:T(8,128)} %bitcast.6, bf16[8,2,16,16,512]{4,3,2,1,0:T(8,128)(2,1)} %pert_hbm.1, s32[1,1024]{1,0:T(1,128)} %bitcast.7, s32[1,1024]{1,0:T(1,128)} %bitcast.8, f32[1,1024]{1,0:T(1,128)} %bitcast.9, f32[1,1024]{1,0:T(1,128)} %bitcast.10), custom_call_target="tpu_custom_call" | custom-call | tf_op jit(solution)/shard_map/pallas_call | solution.py:508
  55.5 1.8 %add.3 = f32[512,128]{1,0:T(8,128)} add(f32[512,128]{1,0:T(8,128)} %get-tuple-element.7, f32[512,128]{1,0:T(8,128)} %get-tuple-element.8) | non-fusion elementwise | flops 65536 | bytes 786432 | tf_op jit(solution)/shard_map/add | solution.py:560

commit v4 on v3

--- a/solution.py
+++ b/solution.py
@@ -49,14 +49,12 @@
 def one_pass(rows, first, last, inside):
     out = {}
     for k in range(first, last + 1):
-        here, above, below = rows.get(k), rows.get(k - 1), rows.get(k + 1)
-        vertical = [v for v in (above, below) if v is not None]
-        beside = vertical[0] if len(vertical) == 1 else vertical[0] + vertical[1] if vertical else None
-        if here is not None:
-            beside = sides(here) if beside is None else beside + sides(here)
-            value = here + diffuse * (beside - 4.0 * here)
-        else:
-            value = diffuse * beside
+        value = None
+        for near in (k - 1, k, k + 1):
+            if near in rows:
+                value = rows[near] if value is None else value + rows[near]
+        if k in rows:
+            value = value + sides(rows[k])
         out[k] = inside(k, value)
     return out
 
@@ -115,8 +113,7 @@
     has_prev = reg > 0
     has_next = reg < regions - 1
     y_peers = [zh * YS + lax.rem(y + d, YS) for d in range(1, YS)]
-    z_up = lax.rem(zh + 1, ZS) * YS + y
-    z_down = lax.rem(zh + ZS - 1, ZS) * YS + y
+    z_peers = [lax.rem(zh + d, ZS) * YS + y for d in range(1, ZS)]
 
     def remote(source, target, index, **where):
         return pltpu.make_async_remote_copy(
@@ -162,7 +159,7 @@
             remote(fbot.at[g], gtop.at[g], first + GROUPS + g, reg=up),
         )
 
-    winds, acrosses, alongs = streams
+    fields_out, along_out = streams[0][0], streams[1][0]
     sums = 4 * CHUNKS + 4 * GROUPS
 
     def y_copies(n):
@@ -171,16 +168,12 @@
             remote(mine, from_y.at[d], sums + 6 * n + d, mem=who) for d, who in enumerate(y_peers)
         ]
 
-    def near(n, turn):
+    def z_copies(n):
         held, from_z = streams[n][2], streams[n][3]
-        side = turn if n == 0 else 1 - turn
-        where = (z_up, z_down)[side]
-        return remote(held, from_z.at[side], sums + 6 * n + 3 + side, mem=where)
-
-    def far(n):
-        from_z, from_far = streams[n][3], streams[n][4]
-        where, side = (z_up, 0) if n == 0 else (z_down, 1)
-        return remote(from_z.at[side], from_far, sums + 6 * n + 5, mem=where)
+        return [
+            remote(held, from_z.at[d], sums + 6 * n + 3 + d, mem=who)
+            for d, who in reversed(list(enumerate(z_peers)))
+        ]
 
     def y_start(n):
         begin(y_copies(n))
@@ -192,17 +185,15 @@
         for d in range(YS - 1):
             total = total + from_y[d]
         held[...] = total
-        begin((near(n, 0), near(n, 1)))
-
-    def z_middle(n):
-        near(n, 0).wait()
-        far(n).start()
+        begin(z_copies(n))
 
     def z_end(n):
-        held, from_z, from_far = streams[n][2:]
-        near(n, 1).wait()
-        far(n).wait()
-        return held[...] + from_z[0] + from_z[1] + from_far[...]
+        held, from_z = streams[n][2:]
+        finish(z_copies(n))
+        total = held[...]
+        for d in range(ZS - 1):
+            total = total + from_z[d]
+        return total
 
     def begin(copies):
         for copy in copies:
@@ -222,7 +213,7 @@
     barrier = pltpu.get_barrier_semaphore()
     for who in (up, down):
         pl.semaphore_signal(barrier, inc=1, device_id={"reg": who}, device_id_type=MESH)
-    for who in y_peers + [z_up, z_down]:
+    for who in y_peers + z_peers:
         pl.semaphore_signal(barrier, inc=1, device_id={"mem": who}, device_id_type=MESH)
     def get_alpha(c):
         at = pl.ds(pl.multiple_of(c * (LB * R), LB * R), LB * R)
@@ -231,7 +222,7 @@
     each(CHUNKS, lambda c: get_alpha(c).start())
     get_pert = pltpu.make_async_copy(pert_hbm, pert, local_sem.at[0])
     get_pert.start()
-    pl.semaphore_wait(barrier, 2 + YS - 1 + 2)
+    pl.semaphore_wait(barrier, 2 + YS - 1 + ZS - 1)
     flat = alpha.reshape(M * L * R, C)
 
     def arrange(c):
@@ -318,7 +309,9 @@
                 q, s = divmod(i, 4)
                 mine, other = ((0.625, 0.375), (0.875, 0.125), (0.875, 0.125), (0.625, 0.375))[s]
                 near = q - 1 if s < 2 else q + 1
-                part[pl.ds(at + i, ROWS, stride=RX), :] = mine * rows[q] + other * rows[near]
+                part[pl.ds(at + i, ROWS, stride=RX), :] = (diffuse * diffuse * mine) * rows[q] + (
+                    diffuse * diffuse * other
+                ) * rows[near]
             high, low = split(part[pl.ds(at, ROWS * RX), :])
             fine = dot(jnp.concatenate([high, low], axis=1), py2[...])
             for k in range(LB):
@@ -352,16 +345,15 @@
         value = dot(fields[...].reshape(4 * LINES, NY), c0t[:, at])
         at_u = value[0:LINES] + value[LINES : 2 * LINES]
         at_v = value[2 * LINES : 3 * LINES] + value[3 * LINES :]
-        winds[0][0:1, at] = over(on * at_u)
-        winds[0][1:2, at] = over(on * at_v)
-        alongs[0][:, at] = over(beside * jnp.where(second, at_v, at_u))
+        fields_out[0:1, at] = over(on * at_u)
+        fields_out[1:2, at] = over(on * at_v)
+        along_out[:, at] = over(beside * jnp.where(second, at_v, at_u))
         value = dot(fields[0:2].reshape(2 * LINES, NY), c1t[:, at])
-        acrosses[0][:, at] = over(on * (value[0:LINES] + value[LINES:]))
+        fields_out[2:3, at] = over(on * (value[0:LINES] + value[LINES:]))
         return _
 
     lax.fori_loop(0, OBS // NB, pick, 0)
     y_start(0)
-    y_start(1)
     each(GROUPS, lambda g: finish(edges(g)))
     sides_in = [
         jnp.where(has_prev, rtop[...].reshape(GROUPS * EDGE, NY), 0.0),
@@ -369,15 +361,13 @@
     ]
     high, low = split(jnp.concatenate(sides_in, axis=0))
     rim = dot(high, c0t[...]) + dot(low, c0t[...])
-    alongs[0][...] = alongs[0][...] + jnp.sum(rimf[...] * rim, axis=0, keepdims=True)
-    y_start(2)
-
-    for n in range(3):
-        y_end(n)
-    for n in range(3):
-        z_middle(n)
-    (both, slope_y, slope_x) = (z_end(n) * scale for n in range(3))
-    u, v = both[0:1], both[1:2]
+    along_out[...] = along_out[...] + jnp.sum(rimf[...] * rim, axis=0, keepdims=True)
+    y_start(1)
+
+    y_end(0)
+    y_end(1)
+    total, slope_x = z_end(0) * scale, z_end(1) * scale
+    u, v, slope_y = total[0:1], total[1:2], total[2:3]
     is_u, is_v, is_vort, is_adv = kind == 0, kind == 1, kind == 2, kind == 3
     seen = jnp.where(
         is_u,
@@ -455,7 +445,7 @@
                 for t, tap in enumerate(taps):
                     i = 4 * q - 2 + t
                     if 0 <= i < RX:
-                        term = tap * f[i]
+                        term = (diffuse * diffuse * tap) * f[i]
                         value = term if value is None else value + term
                 rows[q] = inside(q, value)
             rows = one_pass(rows, -2, R + 1, inside)
@@ -501,8 +491,7 @@
             one,
             pltpu.VMEM((YS - 1, rows, OBS), F32),
             one,
-            pltpu.VMEM((2, rows, OBS), F32),
-            one,
+            pltpu.VMEM((ZS - 1, rows, OBS), F32),
         )
 
     out, rest = pl.pallas_call(
@@ -530,7 +519,7 @@
             edge,
             edge,
             edge,
-            tuple(stream(rows) for rows in (2, 1, 1)),
+            tuple(stream(rows) for rows in (3, 1)),
             pltpu.VMEM((4 * LINES, OBS), BF16),
             pltpu.VMEM((2 * LINES, OBS), BF16),
             edge,
@@ -543,11 +532,11 @@
             rows3,
             rows3,
             pltpu.SemaphoreType.DMA((1 + CHUNKS,)),
-            pltpu.SemaphoreType.DMA((4 * CHUNKS + 4 * GROUPS + 18,)),
-            pltpu.SemaphoreType.DMA((4 * CHUNKS + 4 * GROUPS + 18,)),
+            pltpu.SemaphoreType.DMA((4 * CHUNKS + 4 * GROUPS + 12,)),
+            pltpu.SemaphoreType.DMA((4 * CHUNKS + 4 * GROUPS + 12,)),
         ],
         compiler_params=pltpu.CompilerParams(
-            collective_id=0, has_side_effects=True, vmem_limit_bytes=56 * 1024 * 1024
+            collective_id=0, has_side_effects=True, vmem_limit_bytes=62 * 1024 * 1024
         ),
     )(
         alpha.reshape(M, L * R, C),

time: 57.4 us -> 55.1 us (0.960)
  Pallas kernels: 55.5 us -> 53.2 us
    pallas_call x1, Pallas kernels: 55.5 us -> 53.2 us  [local(): pl.pallas_call(functools.partial(kernel, 1.0 / math.sqrt(members), region...]
where the time goes in v4:
time: 55.1 us; the launch traced here: 55 us
  Pallas kernels  53.2 us (97%)
  other arithmetic  1.76 us (3%)
    pallas_call x1, Pallas kernels, local(): pl.pallas_call(functools.partial(kernel, 1.0 / math.sqrt(members), region...  53.2 us
    add x1, other arithmetic, local(): return (out + rest).reshape(M, L, R, C)  1.76 us

profile of v4, /device:TPU:8, one launch (start us, length us, event | category | flops | bytes accessed | tf_op | source)
XLA Modules:
  0.0 55.0 jit_solution(10647177571828212609)
XLA Ops:
  0.0 53.2 %shard_map.64 = (f32[512,128]{1,0:T(8,128)}, f32[512,128]{1,0:T(8,128)}) custom-call(f32[8,64,128]{2,1,0:T(8,128)} %bitcast.6, bf16[8,2,16,16,512]{4,3,2,1,0:T(8,128)(2,1)} %pert_hbm.1, s32[1,1024]{1,0:T(1,128)} %bitcast.7, s32[1,1024]{1,0:T(1,128)} %bitcast.8, f32[1,1024]{1,0:T(1,128)} %bitcast.9, f32[1,1024]{1,0:T(1,128)} %bitcast.10), custom_call_target="tpu_custom_call" | custom-call | tf_op jit(solution)/shard_map/pallas_call | solution.py:497
  53.2 1.8 %add.3 = f32[512,128]{1,0:T(8,128)} add(f32[512,128]{1,0:T(8,128)} %get-tuple-element.7, f32[512,128]{1,0:T(8,128)} %get-tuple-element.8) | non-fusion elementwise | flops 65536 | bytes 786432 | tf_op jit(solution)/shard_map/add | solution.py:549

commit v5 on v4

--- a/solution.py
+++ b/solution.py
@@ -104,6 +104,7 @@
     local_sem,
     send_sem,
     recv_sem,
+    far_sem,
 ):
     mem = lax.axis_index("mem")
     reg = lax.axis_index("reg")
@@ -213,7 +214,8 @@
     barrier = pltpu.get_barrier_semaphore()
     for who in (up, down):
         pl.semaphore_signal(barrier, inc=1, device_id={"reg": who}, device_id_type=MESH)
-    for who in y_peers + z_peers:
+    z_up, z_down = z_peers[0], z_peers[-1]
+    for who in y_peers + [z_up, z_down]:
         pl.semaphore_signal(barrier, inc=1, device_id={"mem": who}, device_id_type=MESH)
     def get_alpha(c):
         at = pl.ds(pl.multiple_of(c * (LB * R), LB * R), LB * R)
@@ -222,7 +224,8 @@
     each(CHUNKS, lambda c: get_alpha(c).start())
     get_pert = pltpu.make_async_copy(pert_hbm, pert, local_sem.at[0])
     get_pert.start()
-    pl.semaphore_wait(barrier, 2 + YS - 1 + ZS - 1)
+    pl.semaphore_wait(barrier, 2 + YS - 1 + 2)
+    pl.semaphore_signal(far_sem, inc=1, device_id={"mem": z_down}, device_id_type=MESH)
     flat = alpha.reshape(M * L * R, C)
 
     def arrange(c):
@@ -364,6 +367,7 @@
     along_out[...] = along_out[...] + jnp.sum(rimf[...] * rim, axis=0, keepdims=True)
     y_start(1)
 
+    pl.semaphore_wait(far_sem, 1)
     y_end(0)
     y_end(1)
     total, slope_x = z_end(0) * scale, z_end(1) * scale
@@ -534,6 +538,7 @@
             pltpu.SemaphoreType.DMA((1 + CHUNKS,)),
             pltpu.SemaphoreType.DMA((4 * CHUNKS + 4 * GROUPS + 12,)),
             pltpu.SemaphoreType.DMA((4 * CHUNKS + 4 * GROUPS + 12,)),
+            pltpu.SemaphoreType.REGULAR,
         ],
         compiler_params=pltpu.CompilerParams(
             collective_id=0, has_side_effects=True, vmem_limit_bytes=62 * 1024 * 1024

time: 55.1 us -> 55 us (level)
  no operation moved by 1% of the time
where the time goes in v5:
time: 55 us; the launch traced here: 54.9 us
  Pallas kernels  53.1 us (97%)
  other arithmetic  1.76 us (3%)
    pallas_call x1, Pallas kernels, local(): pl.pallas_call(functools.partial(kernel, 1.0 / math.sqrt(members), region...  53.1 us
    add x1, other arithmetic, local(): return (out + rest).reshape(M, L, R, C)  1.76 us

profile of v5, /device:TPU:8, one launch (start us, length us, event | category | flops | bytes accessed | tf_op | source)
XLA Modules:
  0.0 54.9 jit_solution(4096366355587331497)
XLA Ops:
  0.0 53.1 %shard_map.64 = (f32[512,128]{1,0:T(8,128)}, f32[512,128]{1,0:T(8,128)}) custom-call(f32[8,64,128]{2,1,0:T(8,128)} %bitcast.6, bf16[8,2,16,16,512]{4,3,2,1,0:T(8,128)(2,1)} %pert_hbm.1, s32[1,1024]{1,0:T(1,128)} %bitcast.7, s32[1,1024]{1,0:T(1,128)} %bitcast.8, f32[1,1024]{1,0:T(1,128)} %bitcast.9, f32[1,1024]{1,0:T(1,128)} %bitcast.10), custom_call_target="tpu_custom_call" | custom-call | tf_op jit(solution)/shard_map/pallas_call | solution.py:501
  53.1 1.8 %add.3 = f32[512,128]{1,0:T(8,128)} add(f32[512,128]{1,0:T(8,128)} %get-tuple-element.7, f32[512,128]{1,0:T(8,128)} %get-tuple-element.8) | non-fusion elementwise | flops 65536 | bytes 786432 | tf_op jit(solution)/shard_map/add | solution.py:554

commit v6 on v5

--- a/solution.py
+++ b/solution.py
@@ -64,6 +64,12 @@
     regions,
     alpha_hbm,
     pert_hbm,
+    cell_hbm,
+    kind_hbm,
+    val_hbm,
+    wt_hbm,
+    out_hbm,
+    rest_hbm,
     cell_ref,
     kind_ref,
     val_ref,
@@ -224,6 +230,13 @@
     each(CHUNKS, lambda c: get_alpha(c).start())
     get_pert = pltpu.make_async_copy(pert_hbm, pert, local_sem.at[0])
     get_pert.start()
+    get_obs = [
+        pltpu.make_async_copy(source, target, local_sem.at[1 + CHUNKS + n])
+        for n, (source, target) in enumerate(
+            ((cell_hbm, cell_ref), (kind_hbm, kind_ref), (val_hbm, val_ref), (wt_hbm, wt_ref))
+        )
+    ]
+    begin(get_obs)
     pl.semaphore_wait(barrier, 2 + YS - 1 + 2)
     pl.semaphore_signal(far_sem, inc=1, device_id={"mem": z_down}, device_id_type=MESH)
     flat = alpha.reshape(M * L * R, C)
@@ -239,6 +252,7 @@
 
     each(CHUNKS, arrange)
 
+    finish(get_obs)
     cell = cell_ref[...]
     kind = kind_ref[...]
     column = cell & (NY - 1)
@@ -466,6 +480,8 @@
             begin(rims_out(c))
 
     each(GROUPS, project)
+    put_out = pltpu.make_async_copy(out_ref, out_hbm, local_sem.at[0])
+    put_out.start()
 
     def collect(c):
         finish(rims_out(c))
@@ -480,11 +496,14 @@
                 rest_ref[pl.ds((c * LB + k) * R + r, M, stride=L * R), :] = value
 
     each(CHUNKS, collect)
+    put_rest = pltpu.make_async_copy(rest_ref, rest_hbm, local_sem.at[1])
+    put_rest.start()
+    put_out.wait()
+    put_rest.wait()
 
 
 def local(regions, members, alpha, perturbation, obs_cell, obs_kind, obs_value, obs_weight):
     any_space = pl.BlockSpec(memory_space=pl.ANY)
-    in_vmem = pl.BlockSpec(memory_space=pltpu.VMEM)
     row = (1, OBS)
     edge = pltpu.VMEM((GROUPS, EDGE, NY), F32)
     rows3 = pltpu.VMEM((3, M * L, C), F32)
@@ -501,9 +520,15 @@
     out, rest = pl.pallas_call(
         functools.partial(kernel, 1.0 / math.sqrt(members), regions),
         out_shape=[jax.ShapeDtypeStruct((M * L * R, C), F32)] * 2,
-        in_specs=[any_space, any_space] + [in_vmem] * 4,
-        out_specs=[in_vmem] * 2,
+        in_specs=[any_space] * 6,
+        out_specs=[any_space] * 2,
         scratch_shapes=[
+            pltpu.VMEM(row, I32),
+            pltpu.VMEM(row, I32),
+            pltpu.VMEM(row, F32),
+            pltpu.VMEM(row, F32),
+            pltpu.VMEM((M * L * R, C), F32),
+            pltpu.VMEM((M * L * R, C), F32),
             pltpu.VMEM((M, 2, L, RX, NY), BF16),
             pltpu.VMEM((M, L * R, C), F32),
             pltpu.VMEM((R + 6, M * L, C), F32),
@@ -535,7 +560,7 @@
             rows3,
             rows3,
             rows3,
-            pltpu.SemaphoreType.DMA((1 + CHUNKS,)),
+            pltpu.SemaphoreType.DMA((1 + CHUNKS + 4,)),
             pltpu.SemaphoreType.DMA((4 * CHUNKS + 4 * GROUPS + 12,)),
             pltpu.SemaphoreType.DMA((4 * CHUNKS + 4 * GROUPS + 12,)),
             pltpu.SemaphoreType.REGULAR,

time: 55 us -> 54.2 us (0.985)
  Pallas kernels: 53.1 us -> 52.3 us
    pallas_call x1, Pallas kernels: 53.1 us -> 52.3 us  [local(): pl.pallas_call(functools.partial(kernel, 1.0 / math.sqrt(members), region...]
where the time goes in v6:
time: 54.2 us; the launch traced here: 54 us
  Pallas kernels  52.3 us (96%)
  other arithmetic  1.76 us (3%)
    pallas_call x1, Pallas kernels, local(): pl.pallas_call(functools.partial(kernel, 1.0 / math.sqrt(members), region...  52.3 us
    add x1, other arithmetic, local(): return (out + rest).reshape(M, L, R, C)  1.76 us

profile of v6, /device:TPU:8, one launch (start us, length us, event | category | flops | bytes accessed | tf_op | source)
XLA Modules:
  0.0 54.0 jit_solution(12378727919768745243)
XLA Ops:
  0.0 52.3 %shard_map.64 = (f32[512,128]{1,0:T(8,128)}, f32[512,128]{1,0:T(8,128)}) custom-call(f32[8,64,128]{2,1,0:T(8,128)} %bitcast.6, bf16[8,2,16,16,512]{4,3,2,1,0:T(8,128)(2,1)} %pert_hbm.1, s32[1,1024]{1,0:T(1,128)} %bitcast.7, s32[1,1024]{1,0:T(1,128)} %bitcast.8, f32[1,1024]{1,0:T(1,128)} %bitcast.9, f32[1,1024]{1,0:T(1,128)} %bitcast.10), custom_call_target="tpu_custom_call" | custom-call | tf_op jit(solution)/shard_map/pallas_call | solution.py:520
  52.3 1.8 %add.3 = f32[512,128]{1,0:T(8,128)} add(f32[512,128]{1,0:T(8,128)} %get-tuple-element.7, f32[512,128]{1,0:T(8,128)} %get-tuple-element.8) | non-fusion elementwise | flops 65536 | bytes 786432 | tf_op jit(solution)/shard_map/add | solution.py:579
